TPU v7x, 768 devices: a whole 4x8x12 slice. The times are simulated.
768 devices in a mesh: ma: 12 (over z), row: 64 (over x, y, core).
Axes of the slice: x: 4, y: 8, z: 12, core: 2. Of those that a mesh axis runs over, the one named last changes fastest.
Arguments:
- spectra: float32 [64, 3, 264, 513, 2], P('row', None, 'ma'), may hold values from -0.125 to 0.125
- legendre: bfloat16 [264, 513, 384], P('ma'), may hold values from -0.25 to 0.25
- pair_slots: int32 [264], replicated, may hold values from 0 to 263, each once
- theta_owner: int32 [384], replicated, may hold values from 0 to 383, each once
Outputs:
- flux_grid: bfloat16 [64, 768, 2, 1536], P('row', 'ma')
- flux_spectra: float32 [64, 2, 264, 513, 2], P('row', None, 'ma')
Inputs may be any that keep to these rules, and one draw needn't show every extreme that they name: `pair_slots`: A value p below 256 puts the orders p and 511 - p in that slot; values of 256 or more mark empty slots. `theta_owner`: index d of ma owns the northern rows at positions d * 32 to (d + 1) * 32 - 1 and their mirror rows.
All inputs are finite; a program needn't handle non-finite values.
Results may differ from a plain program's by a relative error of at most 0.0077.
Values may be sent and summed in bfloat16 or wider, within the bound.
No kernel may reach another device: no remote copies, remote signals or barrier semaphores. Data moves between devices by JAX's collectives and lax.ppermute only.
A program may use at most 128 MiB of HBM per device.

v0:
```python
import math

import jax
import jax.numpy as jnp
import numpy as np
from jax import lax
from jax.experimental import pallas as pl
from jax.experimental.pallas import tpu as pltpu
from jax.sharding import PartitionSpec as P

LMAX = 511
NPHI = 1536
NPAIRS = 256
PACK = 513
LANES = 128
TILES = -(-PACK // LANES)
FULL = PACK // LANES * LANES
BF16 = jnp.bfloat16
F32 = jnp.float32
HIGH = lax.Precision.HIGHEST
NT = (((1,), (1,)), ((), ()))


def chebyshev_pair(levels):
    index = np.arange(levels)
    cosines = np.cos(np.pi * (np.outer(index, index) % (2 * (levels - 1))) / (levels - 1))
    ends = np.where((index == 0) | (index == levels - 1), 0.5, 1.0)
    analysis = (2.0 / (levels - 1)) ** 0.5 * np.outer(ends, ends) * cosines
    return cosines.astype(np.float32), analysis.astype(np.float32)


def one_hot(theta_row):
    half = theta_row.shape[1]
    natural = lax.broadcasted_iota(jnp.int32, (half, half), 0)
    return jnp.where(natural == theta_row, 1.0, 0.0).astype(BF16)


def pack_kernel(spectra_ref, out_ref):
    pairs = spectra_ref.shape[0]
    lane = lax.broadcasted_iota(jnp.int32, (2, LANES), 1)
    for i in range(pairs):
        for j in range(TILES - 1):
            out_ref[i * TILES + j] = spectra_ref[i, :, j * LANES : (j + 1) * LANES].astype(BF16)
        last = jnp.broadcast_to(spectra_ref[i, :, FULL:PACK], (2, LANES))
        out_ref[i * TILES + TILES - 1] = jnp.where(lane == 0, last, 0.0).astype(BF16)
    for t in range(pairs * TILES, out_ref.shape[0]):
        out_ref[t] = jnp.zeros((2, LANES), BF16)


def unpack_kernel(tiles_ref, out_ref):
    for i in range(out_ref.shape[0]):
        for j in range(TILES - 1):
            out_ref[i, :, j * LANES : (j + 1) * LANES] = tiles_ref[i * TILES + j].astype(F32)
        out_ref[i, :, FULL:PACK] = tiles_ref[i * TILES + TILES - 1].astype(F32)[:, 0:1]


def slot_masks(pair, column, order_odd):
    used = pair < NPAIRS
    low = jnp.where(used & (column <= LMAX - pair), 1.0, 0.0)
    high = jnp.where(used & (column > LMAX - pair), 1.0, 0.0)
    low_sign = (1 - 2 * (column & 1)).astype(F32)
    high_sign = (1 - 2 * ((column + pair) & 1)).astype(F32)
    return jnp.where(order_odd, high, low), jnp.where(order_odd, high_sign, low_sign)


def synthesis_kernel(pairs_ref, where_ref, tiles_ref, table_ref, theta_ref, out_ref, rows_ref):
    step = pl.program_id(0)
    slots = pl.num_programs(0)
    count = tiles_ref.shape[0]
    owners = out_ref.shape[0]
    own_half = theta_ref.shape[1] // owners
    slot_dev = rows_ref.shape[1] // 24
    pair = pairs_ref[where_ref[0] * slot_dev + step]
    row = lax.broadcasted_iota(jnp.int32, (8, LANES), 0)
    odd = (row & 1) == 1
    field = row >> 1
    lane = lax.broadcasted_iota(jnp.int32, (8, LANES), 1)
    weight = jnp.where((pair == 0) & (row & 1 == 0), 1.0, 2.0)
    blocks = [[], [], [], []]
    for j in range(TILES):
        tiles = [tiles_ref[(f * slot_dev + step) * TILES + j].astype(F32) for f in range(3)]
        mask, sign = slot_masks(pair, lane + j * LANES, odd)
        mask = mask * weight
        for c in range(2):
            parts = [jnp.broadcast_to(t[c : c + 1], (8, LANES)) for t in tiles]
            base = jnp.where(field == 0, parts[0], jnp.where(field == 1, parts[1], parts[2]))
            base = base * mask
            blocks[2 * c].append(base)
            blocks[2 * c + 1].append(base * sign)
    left = jnp.concatenate([jnp.concatenate(b, axis=1) for b in blocks], axis=0)
    sums = jnp.dot(left[:, :FULL].astype(BF16), table_ref[0, :FULL, :], preferred_element_type=F32)
    sums = sums + left[:, FULL : FULL + 1] * table_ref[0, FULL:PACK, :].astype(F32)
    sums = sums.astype(BF16).astype(F32)
    for k in range(4):
        for g in range(rows_ref.shape[0]):
            rows_ref[g, pl.ds(k * 6 * slot_dev + step, 6, stride=slot_dev), :] = sums[
                k * 8 : k * 8 + 6, g * LANES : (g + 1) * LANES
            ]

    @pl.when(step == slots - 1)
    def _():
        select = one_hot(theta_ref[...])
        block = 6 * slot_dev
        moved = []
        for k in range(4):
            rows = jnp.concatenate(
                [rows_ref[g, k * block : (k + 1) * block, :] for g in range(rows_ref.shape[0])],
                axis=1,
            ).astype(BF16)
            moved.append(jnp.dot(rows, select, preferred_element_type=F32))
        for d in range(owners):
            out_ref[d] = jnp.concatenate(
                [m[:, d * own_half : (d + 1) * own_half] for m in moved], axis=1
            ).astype(BF16)


def table_kernel(coarse_cos_ref, coarse_sin_ref, fine_cos_ref, fine_sin_ref, out_ref):
    rows = fine_cos_ref.shape[0]
    fine_cos = fine_cos_ref[...]
    fine_sin = fine_sin_ref[...]
    for a in range(NPHI // LANES):
        cos_a = coarse_cos_ref[:, a : a + 1]
        sin_a = coarse_sin_ref[:, a : a + 1]
        span = slice(a * LANES, (a + 1) * LANES)
        out_ref[0, :, span] = (cos_a * fine_cos - sin_a * fine_sin).astype(BF16)
        out_ref[1, :, span] = (-(sin_a * fine_cos + cos_a * fine_sin)).astype(BF16)


def fourier_kernel(rows_ref, table_ref, flux_ref, out_ref, left_ref, sum_ref):
    step = pl.program_id(0)
    owners = rows_ref.shape[0]
    part = rows_ref.shape[1] // 3
    theta = rows_ref.shape[2] // 2

    @pl.when(step == 0)
    def _():
        turned = [rows_ref[d].astype(F32).T for d in range(owners)]
        for f in range(3):
            for c in range(2):
                left_ref[c, f * theta : (f + 1) * theta, :] = jnp.concatenate(
                    [t[c * theta : (c + 1) * theta, f * part : (f + 1) * part] for t in turned],
                    axis=1,
                ).astype(BF16)
        sum_ref[...] = jnp.zeros_like(sum_ref)

    grid = jnp.dot(left_ref[0], table_ref[0], preferred_element_type=F32)
    grid = grid + jnp.dot(left_ref[1], table_ref[1], preferred_element_type=F32)
    flux = [(grid[:theta] * grid[(1 + g) * theta : (2 + g) * theta]).astype(BF16) for g in range(2)]
    for g in range(2):
        flux_ref[g] = flux[g]
    both = jnp.concatenate(flux, axis=0)
    for c in range(2):
        sum_ref[c] += lax.dot_general(table_ref[c], both, NT, preferred_element_type=F32)

    @pl.when(step == pl.num_programs(0) - 1)
    def _():
        for d in range(owners):
            out_ref[d] = (
                jnp.concatenate([sum_ref[c, d * part : (d + 1) * part, :] for c in range(2)], axis=0)
                * NPHI ** (-0.5)
            ).astype(BF16)


def analysis_kernel(pairs_ref, where_ref, rows_ref, table_ref, theta_ref, out_ref, nat_ref):
    step = pl.program_id(0)
    owners = rows_ref.shape[0]
    own_half = theta_ref.shape[1] // owners
    block = rows_ref.shape[1]
    slot_dev = block // 4
    groups = nat_ref.shape[0]

    @pl.when(step == 0)
    def _():
        select = one_hot(theta_ref[...])
        wide = [rows_ref[d].astype(F32) for d in range(owners)]
        for k in range(4):
            own = jnp.concatenate([w[:, k * own_half : (k + 1) * own_half] for w in wide], axis=1)
            nat = lax.dot_general(own.astype(BF16), select, NT, preferred_element_type=F32)
            for g in range(groups):
                nat_ref[g, k * block : (k + 1) * block, :] = nat[:, g * LANES : (g + 1) * LANES]
        for t in range(2 * slot_dev * TILES, out_ref.shape[0]):
            out_ref[t] = jnp.zeros((2, LANES), BF16)

    left = jnp.concatenate(
        [nat_ref[g, pl.ds(step, 16, stride=slot_dev), :] for g in range(groups)], axis=1
    )
    sums = lax.dot_general(
        left.astype(BF16), table_ref[0, :FULL, :], NT, preferred_element_type=F32
    )
    last = jnp.sum(left * table_ref[0, FULL:PACK, :].astype(F32), axis=1, keepdims=True)
    pair = pairs_ref[where_ref[0] * slot_dev + step]
    row = lax.broadcasted_iota(jnp.int32, (16, LANES), 0)
    odd = (row & 1) == 1
    south = (row & 4) == 4
    lane = lax.broadcasted_iota(jnp.int32, (16, LANES), 1)
    for j in range(TILES):
        mask, sign = slot_masks(pair, lane + j * LANES, odd)
        if j < TILES - 1:
            part = sums[:, j * LANES : (j + 1) * LANES]
        else:
            part = jnp.where(lane == 0, last, 0.0)
        part = part * mask * jnp.where(south, sign, 1.0)
        for g in range(2):
            both = part[g * 8 : g * 8 + 4] + part[g * 8 + 4 : g * 8 + 8]
            tile = jnp.concatenate([both[0:1] + both[1:2], both[2:3] + both[3:4]], axis=0)
            out_ref[(g * slot_dev + step) * TILES + j] = tile.astype(BF16)


def whole(shape):
    return pl.BlockSpec(shape, lambda *_: (0,) * len(shape))


def level_mix(tiles, matrix):
    levels = matrix.shape[0]
    share = tiles.shape[0] // levels
    here = lax.all_to_all(tiles, "row", split_axis=0, concat_axis=0, tiled=True)
    here = here.reshape(levels, share * 2 * LANES).astype(F32)
    mixed = jnp.dot(matrix, here, precision=HIGH).astype(BF16)
    mixed = mixed.reshape(levels * share, 2, LANES)
    return lax.all_to_all(mixed, "row", split_axis=0, concat_axis=0, tiled=True)


def trig_table(pair_slots, owners, slot_dev):
    pairs = pair_slots.reshape(owners, 1, slot_dev)
    orders = jnp.concatenate([pairs, LMAX - pairs], axis=1).reshape(-1, 1)
    span = lax.broadcasted_iota(jnp.int32, (1, LANES), 1)
    coarse = (orders * (span * LANES)) % NPHI
    fine = (orders * span) % NPHI
    scale = 2.0 * math.pi / NPHI
    coarse = coarse.astype(F32) * scale
    fine = fine.astype(F32) * scale
    rows = orders.shape[0]
    return pl.pallas_call(
        table_kernel,
        out_shape=jax.ShapeDtypeStruct((2, rows, NPHI), BF16),
        name="table",
    )(jnp.cos(coarse), jnp.sin(coarse), jnp.cos(fine), jnp.sin(fine))


def local(spectra, legendre, pair_slots, theta_owner):
    slot_dev, _, half = legendre.shape
    owners = lax.axis_size("ma")
    levels = lax.axis_size("row") * spectra.shape[0]
    theta_dev = 2 * half // owners
    groups = half // LANES
    synth_mat, analysis_mat = chebyshev_pair(levels)
    where = lax.axis_index("ma").astype(jnp.int32).reshape(1)
    theta_row = theta_owner.reshape(1, half)
    table = trig_table(pair_slots, owners, slot_dev)

    flat = jnp.transpose(spectra, (0, 1, 2, 4, 3)).reshape(3 * slot_dev, 2, PACK)
    share = -(-3 * slot_dev * TILES // levels)
    tiles = pl.pallas_call(
        pack_kernel,
        out_shape=jax.ShapeDtypeStruct((share * levels, 2, LANES), BF16),
        name="pack",
    )(flat)
    tiles = level_mix(tiles, synth_mat)

    slot_block = pl.BlockSpec((1, PACK, half), lambda s, *_: (s, 0, 0))
    outgoing = pl.pallas_call(
        synthesis_kernel,
        out_shape=jax.ShapeDtypeStruct((owners, 6 * slot_dev, LANES), BF16),
        grid_spec=pltpu.PrefetchScalarGridSpec(
            num_scalar_prefetch=2,
            grid=(slot_dev,),
            in_specs=[whole(tiles.shape), slot_block, whole(theta_row.shape)],
            out_specs=whole((owners, 6 * slot_dev, LANES)),
            scratch_shapes=[pltpu.VMEM((groups, 24 * slot_dev, LANES), F32)],
        ),
        name="synthesis",
    )(pair_slots, where, tiles, legendre, theta_row)
    rows = lax.all_to_all(outgoing, "ma", split_axis=0, concat_axis=0, tiled=True)

    width = 256
    orders = table.shape[1]
    flux, fourier = pl.pallas_call(
        fourier_kernel,
        out_shape=(
            jax.ShapeDtypeStruct((2, theta_dev, NPHI), BF16),
            jax.ShapeDtypeStruct((owners, 4 * slot_dev, 2 * theta_dev), BF16),
        ),
        grid=(NPHI // width,),
        in_specs=[whole(rows.shape), pl.BlockSpec((2, orders, width), lambda q: (0, 0, q))],
        out_specs=(
            pl.BlockSpec((2, theta_dev, width), lambda q: (0, 0, q)),
            whole((owners, 4 * slot_dev, 2 * theta_dev)),
        ),
        scratch_shapes=[
            pltpu.VMEM((2, 3 * theta_dev, orders), BF16),
            pltpu.VMEM((2, orders, 2 * theta_dev), F32),
        ],
        name="fourier",
    )(rows, table)
    returned = lax.all_to_all(fourier, "ma", split_axis=0, concat_axis=0, tiled=True)

    share = -(-2 * slot_dev * TILES // levels)
    tiles = pl.pallas_call(
        analysis_kernel,
        out_shape=jax.ShapeDtypeStruct((share * levels, 2, LANES), BF16),
        grid_spec=pltpu.PrefetchScalarGridSpec(
            num_scalar_prefetch=2,
            grid=(slot_dev,),
            in_specs=[whole(returned.shape), slot_block, whole(theta_row.shape)],
            out_specs=whole((share * levels, 2, LANES)),
            scratch_shapes=[pltpu.VMEM((groups, 16 * slot_dev, LANES), F32)],
        ),
        name="analysis",
    )(pair_slots, where, returned, legendre, theta_row)
    tiles = level_mix(tiles, analysis_mat)
    result = pl.pallas_call(
        unpack_kernel,
        out_shape=jax.ShapeDtypeStruct((2 * slot_dev, 2, PACK), F32),
        name="unpack",
    )(tiles)
    result = jnp.transpose(result.reshape(1, 2, slot_dev, 2, PACK), (0, 1, 2, 4, 3))
    return jnp.transpose(flux, (1, 0, 2))[None], result


def solution(mesh):
    in_specs = (P("row", None, "ma", None, None), P("ma", None, None), P(), P())
    out_specs = (P("row", "ma", None, None), P("row", None, "ma", None, None))
    return jax.shard_map(local, mesh=mesh, in_specs=in_specs, out_specs=out_specs, check_vma=False)
```

profile of v0, /device:TPU:1, one launch (start us, length us, event | category | flops | bytes accessed | tf_op | source)
XLA Modules:
  0.0 175.6 jit_solution(6557000784255582675)
XLA Ops:
  0.6 0.0 copy-start.5
  0.6 1.8 %pack.1 = bf16[384,2,128]{2,1,0:T(2,128)(2,1)} custom-call(f32[66,2,513]{2,1,0:T(2,128)} %bitcast.17), custom_call_target="tpu_custom_call" | custom-call | tf_op jit(solution)/shard_map/pack/pallas_call | solution.py:253
  2.4 25.7 %all_to_all.30 = bf16[384,2,128]{2,1,0:T(2,128)(2,1)S(1)} all-to-all(bf16[384,2,128]{2,1,0:T(2,128)(2,1)} %pack.1), channel_id=1, replica_groups=mesh['ma'=12,'row'=64] {'row'}, dimensions={0} | all-to-all | bytes 393216 | tf_op jit(solution)/shard_map/all_to_all | solution.py:216
  28.1 0.1 reshape.52
  28.2 1.1 convolution_convert_fusion
  29.3 0.7 reshape.53
  30.0 5.7 %all-to-all-start.1 = ((bf16[384,2,128]{2,1,0:T(2,128)(2,1)}), bf16[384,2,128]{2,1,0:T(2,128)(2,1)S(1)}, u32[]{:S(2)}, u32[]{:S(2)}) async-start(bf16[384,2,128]{2,1,0:T(2,128)(2,1)} %reshape.53), calls=%async_computation.1 | async-start | bytes 393216 | tf_op jit(solution)/shard_map/all_to_all | solution.py:220
  35.7 1.3 reshape.54.theta_ref
  37.0 9.7 %all-to-all-done.1.tiles_ref = bf16[384,2,128]{2,1,0:T(2,128)(2,1)S(1)} async-done(((bf16[384,2,128]{2,1,0:T(2,128)(2,1)}), bf16[384,2,128]{2,1,0:T(2,128)(2,1)S(1)}, u32[]{:S(2)}, u32[]{:S(2)}) %all-to-all-start.1) | async-done | bytes 196640 | tf_op jit(solution)/shard_map/all_to_all | solution.py:220
  46.6 0.0 copy-start.1
  46.6 0.7 copy-done.1
  47.3 15.9 %synthesis.1 = bf16[12,132,128]{2,1,0:T(8,128)(2,1)} custom-call(s32[264]{0:T(512)} %pairs_ref.3, s32[1]{0:T(128)} %bitcast.where_ref, bf16[384,2,128]{2,1,0:T(2,128)(2,1)} %copy-done.1, bf16[22,513,384]{2,1,0:T(8,128)(2,1)} %table_ref.3, s32[1,384]{1,0:T(1,128)} %reshape.54.theta_ref), custom_call_target="tpu_custom_call" | custom-call | tf_op jit(solution)/shard_map/synthesis/pallas_call | solution.py:261
  63.2 11.8 %all-to-all-start.2 = ((bf16[12,132,128]{2,1,0:T(8,128)(2,1)}), bf16[12,132,128]{2,1,0:T(8,128)(2,1)S(1)}, u32[]{:S(2)}, u32[]{:S(2)}) async-start(bf16[12,132,128]{2,1,0:T(8,128)(2,1)} %synthesis.1), calls=%async_computation.2 | async-start | bytes 835584 | tf_op jit(solution)/shard_map/all_to_all | solution.py:273
  75.0 0.0 copy-done.5
  75.0 0.1 reshape.55
  75.1 0.1 mul.43
  75.2 3.2 %fusion.11 = (f32[528,128]{1,0:T(8,128)}, f32[528,128]{1,0:T(8,128)}, f32[528,128]{1,0:T(8,128)}, f32[528,128]{1,0:T(8,128)}) fusion(s32[128]{0:T(128)S(1)} %iota_multiply_fusion, s32[528]{0:T(1024)S(1)} %mul.43), kind=kLoop, calls=%fused_computation.17 | loop fusion | flops 1216512 | bytes 1083968 | tf_op jit(solution)/shard_map/sin | solution.py:237
  78.4 0.0 copy-start.4
  78.5 4.8 %table.1.table_ref = bf16[2,528,1536]{2,1,0:T(8,128)(2,1)} custom-call(f32[528,128]{1,0:T(8,128)} %get-tuple-element.9.coarse_cos_ref, f32[528,128]{1,0:T(8,128)} %get-tuple-element.8.coarse_sin_ref, f32[528,128]{1,0:T(8,128)} %get-tuple-element.11.fine_cos_ref, f32[528,128]{1,0:T(8,128)} %get-tuple-element.10.fine_sin_ref), custom_call_target="tpu_custom_call" | custom-call | tf_op jit(solution)/shard_map/table/pallas_call | solution.py:233
  83.2 10.8 %all-to-all-done.2.rows_ref = bf16[12,132,128]{2,1,0:T(8,128)(2,1)S(1)} async-done(((bf16[12,132,128]{2,1,0:T(8,128)(2,1)}), bf16[12,132,128]{2,1,0:T(8,128)(2,1)S(1)}, u32[]{:S(2)}, u32[]{:S(2)}) %all-to-all-start.2) | async-done | bytes 405536 | tf_op jit(solution)/shard_map/all_to_all | solution.py:273
  94.0 0.0 copy-start
  94.0 0.8 copy-done
  94.8 8.3 %fourier.1 = (bf16[2,64,1536]{2,1,0:T(8,128)(2,1)}, bf16[12,88,128]{2,1,0:T(8,128)(2,1)}) custom-call(bf16[12,132,128]{2,1,0:T(8,128)(2,1)} %copy-done, bf16[2,528,1536]{2,1,0:T(8,128)(2,1)} %table.1.table_ref), custom_call_target="tpu_custom_call" | custom-call | tf_op jit(solution)/shard_map/fourier/pallas_call | solution.py:277
  103.1 0.0 copy-start.3
  103.1 18.8 %all_to_all.31.rows_ref = bf16[12,88,128]{2,1,0:T(8,128)(2,1)} all-to-all(bf16[12,88,128]{2,1,0:T(8,128)(2,1)} %get-tuple-element.5), channel_id=1, replica_groups=mesh['ma'=12,'row'=64] {'ma'}, dimensions={0} | all-to-all | bytes 540672 | tf_op jit(solution)/shard_map/all_to_all | solution.py:295
  121.9 16.2 %analysis.1 = bf16[256,2,128]{2,1,0:T(2,128)(2,1)} custom-call(s32[264]{0:T(512)} %pairs_ref.3, s32[1]{0:T(128)} %bitcast.where_ref, bf16[12,88,128]{2,1,0:T(8,128)(2,1)} %all_to_all.31.rows_ref, bf16[22,513,384]{2,1,0:T(8,128)(2,1)} %table_ref.3, s32[1,384]{1,0:T(1,128)} %reshape.54.theta_ref), custom_call_target="tpu_custom_call" | custom-call | tf_op jit(solution)/shard_map/analysis/pallas_call | solution.py:298
  138.1 18.9 %all_to_all.32 = bf16[256,2,128]{2,1,0:T(2,128)(2,1)S(1)} all-to-all(bf16[256,2,128]{2,1,0:T(2,128)(2,1)} %analysis.1), channel_id=1, replica_groups=mesh['ma'=12,'row'=64] {'row'}, dimensions={0} | all-to-all | bytes 262144 | tf_op jit(solution)/shard_map/all_to_all | solution.py:216
  157.0 0.1 reshape.56
  157.1 0.0 copy-done.4
  157.1 0.3 fusion
  157.3 0.7 reshape.57
  158.1 4.9 %all-to-all-start.5 = ((bf16[256,2,128]{2,1,0:T(2,128)(2,1)}), bf16[256,2,128]{2,1,0:T(2,128)(2,1)S(1)}, u32[]{:S(2)}, u32[]{:S(2)}) async-start(bf16[256,2,128]{2,1,0:T(2,128)(2,1)} %reshape.57), calls=%async_computation.5 | async-start | bytes 262144 | tf_op jit(solution)/shard_map/all_to_all | solution.py:220
  162.9 0.0 copy-done.3
  163.0 1.2 copy.8
  164.1 9.2 %all-to-all-done.5.tiles_ref = bf16[256,2,128]{2,1,0:T(2,128)(2,1)S(1)} async-done(((bf16[256,2,128]{2,1,0:T(2,128)(2,1)}), bf16[256,2,128]{2,1,0:T(2,128)(2,1)S(1)}, u32[]{:S(2)}, u32[]{:S(2)}) %all-to-all-start.5) | async-done | bytes 131104 | tf_op jit(solution)/shard_map/all_to_all | solution.py:220
  173.3 0.0 copy-start.2
  173.3 0.6 copy-done.2
  174.0 1.7 unpack.1
  (3 shorter events, 0.0 us)
Async XLA Ops:
  0.6 74.4 %copy-start.5 = (s32[264]{0:T(512)S(1)}, s32[264]{0:T(512)}, u32[]{:S(2)}) copy-start(s32[264]{0:T(512)} %pairs_ref.3) | copy-start | bytes 3172
  30.0 16.7 %all-to-all-start.1 = ((bf16[384,2,128]{2,1,0:T(2,128)(2,1)}), bf16[384,2,128]{2,1,0:T(2,128)(2,1)S(1)}, u32[]{:S(2)}, u32[]{:S(2)}) async-start(bf16[384,2,128]{2,1,0:T(2,128)(2,1)} %reshape.53), calls=%async_computation.1 | async-start | bytes 393216 | tf_op jit(solution)/shard_map/all_to_all | solution.py:220
  46.6 0.7 copy-start.1
  63.2 30.8 %all-to-all-start.2 = ((bf16[12,132,128]{2,1,0:T(8,128)(2,1)}), bf16[12,132,128]{2,1,0:T(8,128)(2,1)S(1)}, u32[]{:S(2)}, u32[]{:S(2)}) async-start(bf16[12,132,128]{2,1,0:T(8,128)(2,1)} %synthesis.1), calls=%async_computation.2 | async-start | bytes 835584 | tf_op jit(solution)/shard_map/all_to_all | solution.py:273
  78.4 78.6 %copy-start.4 = (f32[64,64]{1,0:T(8,128)S(1)}, f32[64,64]{1,0:T(8,128)}, u32[]{:S(2)}) copy-start(f32[64,64]{1,0:T(8,128)} %constant.31.clone) | copy-start | bytes 49156
  94.0 0.8 copy-start
  103.1 59.8 %copy-start.3 = (bf16[2,64,1536]{2,1,0:T(8,128)(2,1)S(1)}, bf16[2,64,1536]{2,1,0:T(8,128)(2,1)}, u32[]{:S(2)}) copy-start(bf16[2,64,1536]{2,1,0:T(8,128)(2,1)} %get-tuple-element.4) | copy-start | bytes 1179652
  158.1 15.2 %all-to-all-start.5 = ((bf16[256,2,128]{2,1,0:T(2,128)(2,1)}), bf16[256,2,128]{2,1,0:T(2,128)(2,1)S(1)}, u32[]{:S(2)}, u32[]{:S(2)}) async-start(bf16[256,2,128]{2,1,0:T(2,128)(2,1)} %reshape.57), calls=%async_computation.5 | async-start | bytes 262144 | tf_op jit(solution)/shard_map/all_to_all | solution.py:220
  173.3 0.7 copy-start.2
where the time goes:
time: 177 us; the launch traced here: 176 us
  blocking collectives  63.4 us (36%)
  Pallas kernels  48.6 us (27%)
  waiting for transfers between devices  29.7 us (17%)
  starting transfers between devices  22.3 us (13%)
  local copies, waits for them, and re-layouts  6.32 us (4%)
  other arithmetic  3.23 us (2%)
    all_to_all x2, blocking collectives, level_mix(): here = lax.all_to_all(tiles, 'row', split_axis=0, concat_axis=0, tiled=True)  44.6 us
    all_to_all x2, waiting for transfers between devices, level_mix(): return lax.all_to_all(mixed, 'row', split_axis=0, concat_axis=0, tiled=True)  18.9 us
    all_to_all x1, blocking collectives, local(): lax.all_to_all(fourier, 'ma', split_axis=0, concat_axis=0, tiled=True)  18.8 us
    pallas_call x1, Pallas kernels, local(): pl.pallas_call(analysis_kernel, out_shape=jax.ShapeDtypeStruct((share * l...  16.2 us
    pallas_call x1, Pallas kernels, local(): pl.pallas_call(synthesis_kernel, out_shape=jax.ShapeDtypeStruct((owners,...  15.9 us
    all_to_all x1, starting transfers between devices, local(): lax.all_to_all(outgoing, 'ma', split_axis=0, concat_axis=0, tiled=True)  11.8 us
    all_to_all x1, waiting for transfers between devices, local(): lax.all_to_all(outgoing, 'ma', split_axis=0, concat_axis=0, tiled=True)  10.8 us
    all_to_all x2, starting transfers between devices, level_mix(): return lax.all_to_all(mixed, 'row', split_axis=0, concat_axis=0, tiled=True)  10.6 us
  transfers between devices with their start and end apart: 3, of which 3 were waited for; matrix products, arithmetic and copies ran while one was open for 3% of the time, Pallas kernels for 3%

commit v1 on v0

v1 whole, which is shorter than its diff:
```python
import math

import jax
import jax.numpy as jnp
import numpy as np
from jax import lax
from jax.experimental import pallas as pl
from jax.experimental.pallas import tpu as pltpu
from jax.sharding import PartitionSpec as P

LMAX = 511
NPHI = 1536
NPAIRS = 256
PACK = 513
LANES = 128
TILES = -(-PACK // LANES)
FULL = PACK // LANES * LANES
WIDTH = 256
SCOPED = 24 << 20
BF16 = jnp.bfloat16
F32 = jnp.float32
HIGH = lax.Precision.HIGHEST
NT = (((1,), (1,)), ((), ()))


def chebyshev_pair(levels):
    index = np.arange(levels)
    cosines = np.cos(np.pi * (np.outer(index, index) % (2 * (levels - 1))) / (levels - 1))
    ends = np.where((index == 0) | (index == levels - 1), 0.5, 1.0)
    analysis = (2.0 / (levels - 1)) ** 0.5 * np.outer(ends, ends) * cosines
    return cosines.astype(np.float32), analysis.astype(np.float32)


def one_hot(theta_row):
    half = theta_row.shape[1]
    natural = lax.broadcasted_iota(jnp.int32, (half, half), 0)
    return jnp.where(natural == theta_row, 1.0, 0.0).astype(BF16)


def pack_kernel(spectra_ref, out_ref):
    pairs = spectra_ref.shape[0]
    lane = lax.broadcasted_iota(jnp.int32, (2, LANES), 1)
    for i in range(pairs):
        for j in range(TILES - 1):
            out_ref[i * TILES + j] = spectra_ref[i, :, j * LANES : (j + 1) * LANES].astype(BF16)
        last = jnp.broadcast_to(spectra_ref[i, :, FULL:PACK], (2, LANES))
        out_ref[i * TILES + TILES - 1] = jnp.where(lane == 0, last, 0.0).astype(BF16)
    for t in range(pairs * TILES, out_ref.shape[0]):
        out_ref[t] = jnp.zeros((2, LANES), BF16)


def unpack_kernel(tiles_ref, out_ref):
    for i in range(out_ref.shape[0]):
        for j in range(TILES - 1):
            out_ref[i, :, j * LANES : (j + 1) * LANES] = tiles_ref[i * TILES + j].astype(F32)
        out_ref[i, :, FULL:PACK] = tiles_ref[i * TILES + TILES - 1].astype(F32)[:, 0:1]


def slot_masks(pair, column, order_odd):
    used = pair < NPAIRS
    low = jnp.where(used & (column <= LMAX - pair), 1.0, 0.0)
    high = jnp.where(used & (column > LMAX - pair), 1.0, 0.0)
    low_sign = (1 - 2 * (column & 1)).astype(F32)
    high_sign = (1 - 2 * ((column + pair) & 1)).astype(F32)
    return jnp.where(order_odd, high, low), jnp.where(order_odd, high_sign, low_sign)


def slot_copy(source_ref, table_ref, arrived, slot):
    return pltpu.make_async_copy(source_ref.at[slot], table_ref.at[slot], arrived.at[slot])


def synthesis_kernel(
    pairs_ref, where_ref, source_ref, tiles_ref, theta_ref, out_ref, rows_ref, table_ref, arrived
):
    slots = table_ref.shape[0]
    for slot in range(slots):
        slot_copy(source_ref, table_ref, arrived, slot).start()
    owners = out_ref.shape[0]
    own_half = theta_ref.shape[1] // owners
    groups = rows_ref.shape[0]
    block = 6 * slots
    row = lax.broadcasted_iota(jnp.int32, (8, LANES), 0)
    odd = (row & 1) == 1
    field = row >> 1
    lane = lax.broadcasted_iota(jnp.int32, (8, LANES), 1)

    def one_slot(slot, carry):
        pair = pairs_ref[where_ref[0] * slots + slot]
        weight = jnp.where((pair == 0) & (row & 1 == 0), 1.0, 2.0)
        blocks = [[], [], [], []]
        for j in range(TILES):
            tiles = [tiles_ref[(f * slots + slot) * TILES + j].astype(F32) for f in range(3)]
            mask, sign = slot_masks(pair, lane + j * LANES, odd)
            mask = mask * weight
            for c in range(2):
                parts = [jnp.broadcast_to(t[c : c + 1], (8, LANES)) for t in tiles]
                base = jnp.where(field == 0, parts[0], jnp.where(field == 1, parts[1], parts[2]))
                base = base * mask
                blocks[2 * c].append(base)
                blocks[2 * c + 1].append(base * sign)
        left = jnp.concatenate([jnp.concatenate(b, axis=1) for b in blocks], axis=0)
        slot_copy(source_ref, table_ref, arrived, slot).wait()
        sums = jnp.dot(
            left[:, :FULL].astype(BF16), table_ref[slot, :FULL, :], preferred_element_type=F32
        )
        sums = sums + left[:, FULL : FULL + 1] * table_ref[slot, FULL:PACK, :].astype(F32)
        for k in range(4):
            for g in range(groups):
                rows_ref[g, pl.ds(k * block + slot, 6, stride=slots), :] = sums[
                    k * 8 : k * 8 + 6, g * LANES : (g + 1) * LANES
                ]
        return carry

    lax.fori_loop(0, slots, one_slot, None, unroll=2)
    select = one_hot(theta_ref[...])
    moved = []
    for k in range(4):
        rows = jnp.concatenate(
            [rows_ref[g, k * block : (k + 1) * block, :] for g in range(groups)], axis=1
        ).astype(BF16)
        moved.append(jnp.dot(rows, select, preferred_element_type=F32))
    for d in range(owners):
        out_ref[d] = jnp.concatenate(
            [m[:, d * own_half : (d + 1) * own_half] for m in moved], axis=1
        ).astype(BF16)


def table_kernel(coarse_cos_ref, coarse_sin_ref, fine_cos_ref, fine_sin_ref, out_ref):
    rows = fine_cos_ref.shape[0]
    fine_cos = fine_cos_ref[...]
    fine_sin = fine_sin_ref[...]
    for a in range(NPHI // LANES):
        cos_a = coarse_cos_ref[:, a : a + 1]
        sin_a = coarse_sin_ref[:, a : a + 1]
        span = slice(a * LANES, (a + 1) * LANES)
        out_ref[:rows, span] = (cos_a * fine_cos - sin_a * fine_sin).astype(BF16)
        out_ref[rows:, span] = (-(sin_a * fine_cos + cos_a * fine_sin)).astype(BF16)


def fourier_kernel(rows_ref, table_ref, flux_ref, out_ref, left_ref, both_ref, sum_ref):
    owners = rows_ref.shape[0]
    part = rows_ref.shape[1] // 3
    theta = rows_ref.shape[2] // 2
    orders = owners * part
    wide = [rows_ref[d].astype(F32) for d in range(owners)]
    for f in range(3):
        turned = jnp.concatenate([w[f * part : (f + 1) * part] for w in wide], axis=0).T
        left_ref[f * theta : (f + 1) * theta, :] = jnp.concatenate(
            [turned[:theta], turned[theta:]], axis=1
        ).astype(BF16)
    for q in range(NPHI // WIDTH):
        span = slice(q * WIDTH, (q + 1) * WIDTH)
        grid = jnp.dot(left_ref[...], table_ref[:, span], preferred_element_type=F32)
        for g in range(2):
            flux = (grid[:theta] * grid[(1 + g) * theta : (2 + g) * theta]).astype(BF16)
            flux_ref[g, :, span] = flux
            both_ref[g * theta : (g + 1) * theta, span] = flux
    sum_ref[...] = lax.dot_general(
        table_ref[...], both_ref[...], NT, preferred_element_type=F32
    ) * NPHI ** (-0.5)
    for d in range(owners):
        out_ref[d] = jnp.concatenate(
            [sum_ref[c * orders + d * part : c * orders + (d + 1) * part, :] for c in range(2)],
            axis=0,
        ).astype(BF16)


def analysis_kernel(
    pairs_ref, where_ref, source_ref, rows_ref, theta_ref, out_ref, nat_ref, table_ref, arrived
):
    slots = table_ref.shape[0]
    for slot in range(slots):
        slot_copy(source_ref, table_ref, arrived, slot).start()
    owners = rows_ref.shape[0]
    own_half = theta_ref.shape[1] // owners
    block = rows_ref.shape[1]
    groups = nat_ref.shape[0]
    select = one_hot(theta_ref[...])
    wide = [rows_ref[d].astype(F32) for d in range(owners)]
    for k in range(4):
        own = jnp.concatenate([w[:, k * own_half : (k + 1) * own_half] for w in wide], axis=1)
        nat = lax.dot_general(own.astype(BF16), select, NT, preferred_element_type=F32)
        for g in range(groups):
            nat_ref[g, k * block : (k + 1) * block, :] = nat[:, g * LANES : (g + 1) * LANES]
    for t in range(2 * slots * TILES, out_ref.shape[0]):
        out_ref[t] = jnp.zeros((2, LANES), BF16)
    row = lax.broadcasted_iota(jnp.int32, (16, LANES), 0)
    odd = (row & 1) == 1
    south = (row & 4) == 4
    lane = lax.broadcasted_iota(jnp.int32, (16, LANES), 1)

    def one_slot(slot, carry):
        left = jnp.concatenate(
            [nat_ref[g, pl.ds(slot, 16, stride=slots), :] for g in range(groups)], axis=1
        )
        slot_copy(source_ref, table_ref, arrived, slot).wait()
        sums = lax.dot_general(
            left.astype(BF16), table_ref[slot, :FULL, :], NT, preferred_element_type=F32
        )
        last = jnp.sum(left * table_ref[slot, FULL:PACK, :].astype(F32), axis=1, keepdims=True)
        pair = pairs_ref[where_ref[0] * slots + slot]
        for j in range(TILES):
            mask, sign = slot_masks(pair, lane + j * LANES, odd)
            if j < TILES - 1:
                part = sums[:, j * LANES : (j + 1) * LANES]
            else:
                part = jnp.where(lane == 0, last, 0.0)
            part = part * mask * jnp.where(south, sign, 1.0)
            for g in range(2):
                both = part[g * 8 : g * 8 + 4] + part[g * 8 + 4 : g * 8 + 8]
                tile = jnp.concatenate([both[0:1] + both[1:2], both[2:3] + both[3:4]], axis=0)
                out_ref[(g * slots + slot) * TILES + j] = tile.astype(BF16)
        return carry

    lax.fori_loop(0, slots, one_slot, None, unroll=2)


def call(kernel, name, out_shape, operands, scratch=(), scalars=0, remote=0):
    first = scalars + remote
    spaces = [pltpu.SMEM] * scalars + [pltpu.HBM] * remote + [pltpu.VMEM] * (len(operands) - first)
    operands = [
        x if i < first else pltpu.with_memory_space_constraint(x, pltpu.VMEM)
        for i, x in enumerate(operands)
    ]
    return pl.pallas_call(
        kernel,
        out_shape=tuple(pltpu.VMEM(shape, dtype) for shape, dtype in out_shape),
        in_specs=[pl.BlockSpec(memory_space=space) for space in spaces],
        out_specs=(pl.BlockSpec(memory_space=pltpu.VMEM),) * len(out_shape),
        scratch_shapes=scratch,
        compiler_params=pltpu.CompilerParams(vmem_limit_bytes=SCOPED),
        name=name,
    )(*operands)


def level_mix(tiles, matrix, beside=None):
    levels = matrix.shape[0]
    share = tiles.shape[0] // levels
    here = lax.all_to_all(tiles, "row", split_axis=0, concat_axis=0, tiled=True)
    here, beside = lax.optimization_barrier((here, beside))
    here = here.reshape(levels, share * 2 * LANES).astype(F32)
    mixed = jnp.dot(matrix, here, precision=HIGH).astype(BF16)
    mixed = mixed.reshape(levels * share, 2, LANES)
    return lax.all_to_all(mixed, "row", split_axis=0, concat_axis=0, tiled=True), beside


def trig_table(pair_slots, owners, slot_dev):
    pairs = pair_slots.reshape(owners, 1, slot_dev)
    orders = jnp.concatenate([pairs, LMAX - pairs], axis=1).reshape(-1, 1)
    span = lax.broadcasted_iota(jnp.int32, (1, LANES), 1)
    coarse = (orders * (span * LANES)) % NPHI
    fine = (orders * span) % NPHI
    scale = 2.0 * math.pi / NPHI
    coarse = coarse.astype(F32) * scale
    fine = fine.astype(F32) * scale
    shape = (2 * orders.shape[0], NPHI)
    trig = (jnp.cos(coarse), jnp.sin(coarse), jnp.cos(fine), jnp.sin(fine))
    return call(table_kernel, "table", [(shape, BF16)], trig)[0]


def local(spectra, legendre, pair_slots, theta_owner):
    slot_dev, _, half = legendre.shape
    owners = lax.axis_size("ma")
    levels = lax.axis_size("row") * spectra.shape[0]
    theta_dev = 2 * half // owners
    groups = half // LANES
    synth_mat, analysis_mat = chebyshev_pair(levels)
    where = lax.axis_index("ma").astype(jnp.int32).reshape(1)
    theta_row = theta_owner.reshape(1, half)
    table = trig_table(pair_slots, owners, slot_dev)

    held = [pltpu.VMEM(legendre.shape, BF16), pltpu.SemaphoreType.DMA((slot_dev,))]
    flat = jnp.transpose(spectra, (0, 1, 2, 4, 3)).reshape(3 * slot_dev, 2, PACK)
    share = -(-3 * slot_dev * TILES // levels)
    (tiles,) = pl.pallas_call(
        pack_kernel,
        out_shape=(pltpu.VMEM((share * levels, 2, LANES), BF16),),
        out_specs=(pl.BlockSpec(memory_space=pltpu.VMEM),),
        compiler_params=pltpu.CompilerParams(vmem_limit_bytes=SCOPED),
        name="pack",
    )(flat)
    tiles, (table, theta_row) = level_mix(tiles, synth_mat, (table, theta_row))

    (outgoing,) = call(
        synthesis_kernel,
        "synthesis",
        [((owners, 6 * slot_dev, LANES), BF16)],
        (pair_slots, where, legendre, tiles, theta_row),
        [pltpu.VMEM((groups, 24 * slot_dev, LANES), F32)] + held,
        scalars=2,
        remote=1,
    )
    rows = lax.all_to_all(outgoing, "ma", split_axis=0, concat_axis=0, tiled=True)

    orders = table.shape[0]
    flux, fourier = call(
        fourier_kernel,
        "fourier",
        [((2, theta_dev, NPHI), BF16), ((owners, 4 * slot_dev, 2 * theta_dev), BF16)],
        (rows, table),
        [
            pltpu.VMEM((3 * theta_dev, orders), BF16),
            pltpu.VMEM((2 * theta_dev, NPHI), BF16),
            pltpu.VMEM((orders, 2 * theta_dev), F32),
        ],
    )
    returned = lax.all_to_all(fourier, "ma", split_axis=0, concat_axis=0, tiled=True)

    share = -(-2 * slot_dev * TILES // levels)
    (tiles,) = call(
        analysis_kernel,
        "analysis",
        [((share * levels, 2, LANES), BF16)],
        (pair_slots, where, legendre, returned, theta_row),
        [pltpu.VMEM((groups, 16 * slot_dev, LANES), F32)] + held,
        scalars=2,
        remote=1,
    )
    flux = jnp.transpose(flux, (1, 0, 2))[None]
    tiles, flux = level_mix(tiles, analysis_mat, flux)
    tiles = pltpu.with_memory_space_constraint(tiles, pltpu.VMEM)
    result = pl.pallas_call(
        unpack_kernel,
        out_shape=jax.ShapeDtypeStruct((2 * slot_dev, 2, PACK), F32),
        in_specs=[pl.BlockSpec(memory_space=pltpu.VMEM)],
        compiler_params=pltpu.CompilerParams(vmem_limit_bytes=SCOPED),
        name="unpack",
    )(tiles)
    result = jnp.transpose(result.reshape(1, 2, slot_dev, 2, PACK), (0, 1, 2, 4, 3))
    return flux, result


def solution(mesh):
    in_specs = (P("row", None, "ma", None, None), P("ma", None, None), P(), P())
    out_specs = (P("row", "ma", None, None), P("row", None, "ma", None, None))
    return jax.shard_map(local, mesh=mesh, in_specs=in_specs, out_specs=out_specs, check_vma=False)
```

time: 177 us -> 160 us (0.904)
  Pallas kernels: 48.6 us -> 26.6 us
  waiting for transfers between devices: 29.7 us -> 24.2 us
  local copies, waits for them, and re-layouts: 6.32 us -> 11.1 us
  blocking collectives: 63.4 us -> 68.1 us
  starting transfers between devices: 22.3 us -> 25.1 us
    all_to_all x0 -> x1, blocking collectives: none -> 30.8 us  [local(): lax.all_to_all(outgoing, 'ma', split_axis=0, concat_axis=0, tiled=True)]
    all_to_all x2 -> x1, blocking collectives: 44.6 us -> 18.9 us  [level_mix(): here = lax.all_to_all(tiles, 'row', split_axis=0, concat_axis=0, tiled=True)]
    pallas_call x5, Pallas kernels: 46.9 us -> 25.8 us  [the longest x4 25 us: call(): pl.pallas_call(kernel, out_shape=tuple((pltpu.VMEM(shape, dtype) for shap...]
    all_to_all x3, waiting for transfers between devices: 29.7 us -> 24.2 us  [the longest x2 19.1 us: level_mix(): lax.all_to_all(mixed, 'row', split_axis=0, concat_axis=0, tiled=True)]
    unnamed x13 -> x15, local copies, waits for them, and re-layouts: 3.27 us -> 7.31 us
    all_to_all x3, starting transfers between devices: 22.3 us -> 25.1 us  [the longest x1 14.6 us: level_mix(): here = lax.all_to_all(tiles, 'row', split_axis=0, concat_axis=0, tiled=True)]
  transfers between devices with their start and end apart: 3 -> 3, of which waited for: 3 -> 3; matrix products, arithmetic and copies ran while one was open for 3% -> 4% of each run, Pallas kernels for 3% -> 1%
where the time goes in v1:
time: 160 us
  blocking collectives  68.1 us (43%)
  Pallas kernels  26.6 us (17%)
  starting transfers between devices  25.1 us (16%)
  waiting for transfers between devices  24.2 us (15%)
  local copies, waits for them, and re-layouts  11.1 us (7%)
  other arithmetic  2.27 us (1%)
    all_to_all x1, blocking collectives, local(): lax.all_to_all(outgoing, 'ma', split_axis=0, concat_axis=0, tiled=True)  30.8 us
    pallas_call x4, Pallas kernels, call(): pl.pallas_call(kernel, out_shape=tuple((pltpu.VMEM(shape, dtype) for shap...  25 us
    all_to_all x2, waiting for transfers between devices, level_mix(): lax.all_to_all(mixed, 'row', split_axis=0, concat_axis=0, tiled=True)  19.1 us
    all_to_all x1, blocking collectives, level_mix(): here = lax.all_to_all(tiles, 'row', split_axis=0, concat_axis=0, tiled=True)  18.9 us
    all_to_all x1, blocking collectives, local(): lax.all_to_all(fourier, 'ma', split_axis=0, concat_axis=0, tiled=True)  18.4 us
    all_to_all x1, starting transfers between devices, level_mix(): here = lax.all_to_all(tiles, 'row', split_axis=0, concat_axis=0, tiled=True)  14.6 us
    all_to_all x2, starting transfers between devices, level_mix(): lax.all_to_all(mixed, 'row', split_axis=0, concat_axis=0, tiled=True)  10.6 us
    unnamed x15, local copies, waits for them, and re-layouts  7.31 us
  transfers between devices with their start and end apart: 3, of which 3 were waited for; matrix products, arithmetic and copies ran while one was open for 4% of the time, Pallas kernels for 1%

profile of v1, /device:TPU:1, one launch (start us, length us, event | category | flops | bytes accessed | tf_op | source)
XLA Modules:
  0.0 159.7 jit_solution(8491133712446469908)
XLA Ops:
  0.6 0.0 copy-start.3
  0.6 1.0 copy-done.3
  1.6 0.8 pack.1
  2.4 14.6 %all-to-all-start = ((bf16[384,2,128]{2,1,0:T(2,128)(2,1)}), bf16[384,2,128]{2,1,0:T(2,128)(2,1)S(1)}, u32[]{:S(2)}, u32[]{:S(2)}) async-start(bf16[384,2,128]{2,1,0:T(2,128)(2,1)} %pack.1), calls=%async_computation | async-start | bytes 393216 | tf_op jit(solution)/shard_map/all_to_all | solution.py:239
  17.0 0.8 reshape.52
  17.8 0.1 mul.43
  17.9 0.7 reshape.53.theta_ref
  18.6 2.2 %fusion.12 = (f32[528,128]{1,0:T(8,128)S(1)}, f32[528,128]{1,0:T(8,128)S(1)}, f32[528,128]{1,0:T(8,128)S(1)}, f32[528,128]{1,0:T(8,128)S(1)}) fusion(s32[128]{0:T(128)S(1)} %iota_multiply_fusion, s32[528]{0:T(1024)S(1)} %mul.43), kind=kLoop, calls=%fused_computation.18 | loop fusion | flops 1216512 | bytes 1083968 | tf_op jit(solution)/shard_map/sin | solution.py:257
  20.9 2.1 %table.1.table_ref = bf16[1056,1536]{1,0:T(8,128)(2,1)S(1)} custom-call(f32[528,128]{1,0:T(8,128)S(1)} %get-tuple-element.19.coarse_cos_ref, f32[528,128]{1,0:T(8,128)S(1)} %get-tuple-element.18.coarse_sin_ref, f32[528,128]{1,0:T(8,128)S(1)} %get-tuple-element.21.fine_cos_ref, f32[528,128]{1,0:T(8,128)S(1)} %get-tuple-element.20.fine_sin_ref), custom_call_target="tpu_custom_call" | custom-call | tf_op jit(solution)/shard_map/table/pallas_call | solution.py:225
  23.0 0.0 copy-start.5
  23.0 5.0 %all-to-all-done = bf16[384,2,128]{2,1,0:T(2,128)(2,1)S(1)} async-done(((bf16[384,2,128]{2,1,0:T(2,128)(2,1)}), bf16[384,2,128]{2,1,0:T(2,128)(2,1)S(1)}, u32[]{:S(2)}, u32[]{:S(2)}) %all-to-all-start) | async-done | bytes 196640 | tf_op jit(solution)/shard_map/all_to_all | solution.py:239
  28.1 0.8 reshape.54
  28.8 1.2 fusion
  30.0 0.7 reshape.55
  30.8 5.7 %all-to-all-start.1 = ((bf16[384,2,128]{2,1,0:T(2,128)(2,1)}), bf16[384,2,128]{2,1,0:T(2,128)(2,1)S(1)}, u32[]{:S(2)}, u32[]{:S(2)}) async-start(bf16[384,2,128]{2,1,0:T(2,128)(2,1)} %reshape.55), calls=%async_computation.1 | async-start | bytes 393216 | tf_op jit(solution)/shard_map/all_to_all | solution.py:244
  36.5 10.9 %all-to-all-done.1.tiles_ref = bf16[384,2,128]{2,1,0:T(2,128)(2,1)S(1)} async-done(((bf16[384,2,128]{2,1,0:T(2,128)(2,1)}), bf16[384,2,128]{2,1,0:T(2,128)(2,1)S(1)}, u32[]{:S(2)}, u32[]{:S(2)}) %all-to-all-start.1) | async-done | bytes 196640 | tf_op jit(solution)/shard_map/all_to_all | solution.py:244
  47.4 0.0 copy-start
  47.4 3.5 %copy-done = bf16[22,513,384]{2,1,0:T(8,128)(2,1)S(1)} copy-done((bf16[22,513,384]{2,1,0:T(8,128)(2,1)S(1)}, bf16[22,513,384]{2,1,0:T(8,128)(2,1)}, u32[]{:S(2)}) %copy-start) | copy-done | bytes 8667672
  50.9 0.0 copy-start.4
  50.9 0.7 copy-done.4
  51.6 0.0 copy-start.1
  51.6 10.2 %synthesis.1 = bf16[12,132,128]{2,1,0:T(8,128)(2,1)S(1)} custom-call(s32[264]{0:T(512)S(1)} %copy-done.4, s32[1]{0:T(128)} %bitcast.where_ref, bf16[22,513,384]{2,1,0:T(8,128)(2,1)S(1)} %copy-done, bf16[384,2,128]{2,1,0:T(2,128)(2,1)S(1)} %all-to-all-done.1.tiles_ref, s32[1,384]{1,0:T(1,128)S(1)} %reshape.53.theta_ref), custom_call_target="tpu_custom_call" | custom-call | tf_op jit(solution)/shard_map/synthesis/pallas_call | solution.py:225
  61.8 0.0 copy-start.6
  61.8 30.8 %all_to_all.30.rows_ref = bf16[12,132,128]{2,1,0:T(8,128)(2,1)S(1)} all-to-all(bf16[12,132,128]{2,1,0:T(8,128)(2,1)S(1)} %synthesis.1), channel_id=1, replica_groups=mesh['ma'=12,'row'=64] {'ma'}, dimensions={0} | all-to-all | bytes 811008 | tf_op jit(solution)/shard_map/all_to_all | solution.py:293
  92.6 2.1 %fourier.1 = (bf16[2,64,1536]{2,1,0:T(8,128)(2,1)S(1)}, bf16[12,88,128]{2,1,0:T(8,128)(2,1)S(1)}) custom-call(bf16[12,132,128]{2,1,0:T(8,128)(2,1)S(1)} %all_to_all.30.rows_ref, bf16[1056,1536]{1,0:T(8,128)(2,1)S(1)} %table.1.table_ref), custom_call_target="tpu_custom_call" | custom-call | tf_op jit(solution)/shard_map/fourier/pallas_call | solution.py:225
  94.6 0.0 copy-start.2
  94.7 18.4 %all_to_all.31.rows_ref = bf16[12,88,128]{2,1,0:T(8,128)(2,1)S(1)} all-to-all(bf16[12,88,128]{2,1,0:T(8,128)(2,1)S(1)} %get-tuple-element.12), channel_id=1, replica_groups=mesh['ma'=12,'row'=64] {'ma'}, dimensions={0} | all-to-all | bytes 540672 | tf_op jit(solution)/shard_map/all_to_all | solution.py:307
  113.0 0.0 copy-done.5
  113.0 0.0 copy-done.1
  113.0 10.6 %analysis.1 = bf16[256,2,128]{2,1,0:T(2,128)(2,1)S(1)} custom-call(s32[264]{0:T(512)S(1)} %copy-done.5, s32[1]{0:T(128)} %bitcast.where_ref, bf16[22,513,384]{2,1,0:T(8,128)(2,1)S(1)} %copy-done.1, bf16[12,88,128]{2,1,0:T(8,128)(2,1)S(1)} %all_to_all.31.rows_ref, s32[1,384]{1,0:T(1,128)S(1)} %reshape.53.theta_ref), custom_call_target="tpu_custom_call" | custom-call | tf_op jit(solution)/shard_map/analysis/pallas_call | solution.py:225
  123.7 18.9 %all_to_all.32 = bf16[256,2,128]{2,1,0:T(2,128)(2,1)S(1)} all-to-all(bf16[256,2,128]{2,1,0:T(2,128)(2,1)S(1)} %analysis.1), channel_id=1, replica_groups=mesh['ma'=12,'row'=64] {'row'}, dimensions={0} | all-to-all | bytes 262144 | tf_op jit(solution)/shard_map/all_to_all | solution.py:239
  142.6 0.0 copy-done.2
  142.6 0.1 reshape.56
  142.7 0.0 copy-done.6
  142.7 0.3 fusion.1
  142.9 0.7 reshape.57
  143.7 4.9 %all-to-all-start.5 = ((bf16[256,2,128]{2,1,0:T(2,128)(2,1)}), bf16[256,2,128]{2,1,0:T(2,128)(2,1)S(1)}, u32[]{:S(2)}, u32[]{:S(2)}) async-start(bf16[256,2,128]{2,1,0:T(2,128)(2,1)} %reshape.57), calls=%async_computation.5 | async-start | bytes 262144 | tf_op jit(solution)/shard_map/all_to_all | solution.py:244
  148.6 2.1 %copy.8 = bf16[1,64,2,1536]{3,2,1,0:T(2,128)(2,1)} copy(bf16[1,64,2,1536]{3,1,2,0:T(8,128)(2,1)} %bitcast.18) | data formatting | bytes 786432
  150.7 8.2 %all-to-all-done.5.tiles_ref = bf16[256,2,128]{2,1,0:T(2,128)(2,1)S(1)} async-done(((bf16[256,2,128]{2,1,0:T(2,128)(2,1)}), bf16[256,2,128]{2,1,0:T(2,128)(2,1)S(1)}, u32[]{:S(2)}, u32[]{:S(2)}) %all-to-all-start.5) | async-done | bytes 131104 | tf_op jit(solution)/shard_map/all_to_all | solution.py:244
  158.9 0.8 unpack.1
  (3 shorter events, 0.0 us)
Async XLA Ops:
  0.6 1.0 copy-start.3
  2.4 25.6 %all-to-all-start = ((bf16[384,2,128]{2,1,0:T(2,128)(2,1)}), bf16[384,2,128]{2,1,0:T(2,128)(2,1)S(1)}, u32[]{:S(2)}, u32[]{:S(2)}) async-start(bf16[384,2,128]{2,1,0:T(2,128)(2,1)} %pack.1), calls=%async_computation | async-start | bytes 393216 | tf_op jit(solution)/shard_map/all_to_all | solution.py:239
  23.0 90.0 %copy-start.5 = (s32[264]{0:T(512)S(1)}, s32[264]{0:T(512)}, u32[]{:S(2)}) copy-start(s32[264]{0:T(512)} %pairs_ref.3) | copy-start | bytes 3172
  30.8 16.6 %all-to-all-start.1 = ((bf16[384,2,128]{2,1,0:T(2,128)(2,1)}), bf16[384,2,128]{2,1,0:T(2,128)(2,1)S(1)}, u32[]{:S(2)}, u32[]{:S(2)}) async-start(bf16[384,2,128]{2,1,0:T(2,128)(2,1)} %reshape.55), calls=%async_computation.1 | async-start | bytes 393216 | tf_op jit(solution)/shard_map/all_to_all | solution.py:244
  47.4 3.5 %copy-start = (bf16[22,513,384]{2,1,0:T(8,128)(2,1)S(1)}, bf16[22,513,384]{2,1,0:T(8,128)(2,1)}, u32[]{:S(2)}) copy-start(bf16[22,513,384]{2,1,0:T(8,128)(2,1)} %source_ref.3) | copy-start | bytes 26002948
  50.9 0.7 copy-start.4
  51.6 61.5 %copy-start.1 = (bf16[22,513,384]{2,1,0:T(8,128)(2,1)S(1)}, bf16[22,513,384]{2,1,0:T(8,128)(2,1)}, u32[]{:S(2)}) copy-start(bf16[22,513,384]{2,1,0:T(8,128)(2,1)} %source_ref.3) | copy-start | bytes 26002948
  61.8 80.9 %copy-start.6 = (f32[64,64]{1,0:T(8,128)S(1)}, f32[64,64]{1,0:T(8,128)}, u32[]{:S(2)}) copy-start(f32[64,64]{1,0:T(8,128)} %constant.31.clone) | copy-start | bytes 49156
  94.6 48.0 %copy-start.2 = (bf16[2,64,1536]{2,1,0:T(8,128)(2,1)}, bf16[2,64,1536]{2,1,0:T(8,128)(2,1)S(1)}, u32[]{:S(2)}) copy-start(bf16[2,64,1536]{2,1,0:T(8,128)(2,1)S(1)} %get-tuple-element.13) | copy-start | bytes 1179652
  143.7 15.2 %all-to-all-start.5 = ((bf16[256,2,128]{2,1,0:T(2,128)(2,1)}), bf16[256,2,128]{2,1,0:T(2,128)(2,1)S(1)}, u32[]{:S(2)}, u32[]{:S(2)}) async-start(bf16[256,2,128]{2,1,0:T(2,128)(2,1)} %reshape.57), calls=%async_computation.5 | async-start | bytes 262144 | tf_op jit(solution)/shard_map/all_to_all | solution.py:244

commit v2 on v1

--- a/solution.py
+++ b/solution.py
@@ -16,7 +16,9 @@
 TILES = -(-PACK // LANES)
 FULL = PACK // LANES * LANES
 WIDTH = 256
-SCOPED = 24 << 20
+SCOPED = 16 << 20
+SYNTHESIS_SCOPED = 46 << 20
+GROUP = 4
 BF16 = jnp.bfloat16
 F32 = jnp.float32
 HIGH = lax.Precision.HIGHEST
@@ -65,16 +67,16 @@
     return jnp.where(order_odd, high, low), jnp.where(order_odd, high_sign, low_sign)
 
 
-def slot_copy(source_ref, table_ref, arrived, slot):
-    return pltpu.make_async_copy(source_ref.at[slot], table_ref.at[slot], arrived.at[slot])
-
-
 def synthesis_kernel(
-    pairs_ref, where_ref, source_ref, tiles_ref, theta_ref, out_ref, rows_ref, table_ref, arrived
+    pairs_ref, where_ref, source_ref, tiles_ref, theta_ref, out_ref, table_ref, rows_ref, arrived
 ):
     slots = table_ref.shape[0]
-    for slot in range(slots):
-        slot_copy(source_ref, table_ref, arrived, slot).start()
+    copies = [
+        pltpu.make_async_copy(source_ref.at[slot], table_ref.at[slot], arrived.at[slot])
+        for slot in range(slots)
+    ]
+    for copy in copies:
+        copy.start()
     owners = out_ref.shape[0]
     own_half = theta_ref.shape[1] // owners
     groups = rows_ref.shape[0]
@@ -84,7 +86,10 @@
     field = row >> 1
     lane = lax.broadcasted_iota(jnp.int32, (8, LANES), 1)
 
-    def one_slot(slot, carry):
+    for slot in range(slots):
+        if (slot - 2) % GROUP == 0 or slot == 0:
+            for copy in copies[slot : slot + GROUP if slot else 2]:
+                copy.wait()
         pair = pairs_ref[where_ref[0] * slots + slot]
         weight = jnp.where((pair == 0) & (row & 1 == 0), 1.0, 2.0)
         blocks = [[], [], [], []]
@@ -99,7 +104,6 @@
                 blocks[2 * c].append(base)
                 blocks[2 * c + 1].append(base * sign)
         left = jnp.concatenate([jnp.concatenate(b, axis=1) for b in blocks], axis=0)
-        slot_copy(source_ref, table_ref, arrived, slot).wait()
         sums = jnp.dot(
             left[:, :FULL].astype(BF16), table_ref[slot, :FULL, :], preferred_element_type=F32
         )
@@ -109,9 +113,6 @@
                 rows_ref[g, pl.ds(k * block + slot, 6, stride=slots), :] = sums[
                     k * 8 : k * 8 + 6, g * LANES : (g + 1) * LANES
                 ]
-        return carry
-
-    lax.fori_loop(0, slots, one_slot, None, unroll=2)
     select = one_hot(theta_ref[...])
     moved = []
     for k in range(4):
@@ -165,12 +166,8 @@
         ).astype(BF16)
 
 
-def analysis_kernel(
-    pairs_ref, where_ref, source_ref, rows_ref, theta_ref, out_ref, nat_ref, table_ref, arrived
-):
+def analysis_kernel(pairs_ref, where_ref, rows_ref, table_ref, theta_ref, out_ref, nat_ref):
     slots = table_ref.shape[0]
-    for slot in range(slots):
-        slot_copy(source_ref, table_ref, arrived, slot).start()
     owners = rows_ref.shape[0]
     own_half = theta_ref.shape[1] // owners
     block = rows_ref.shape[1]
@@ -189,11 +186,10 @@
     south = (row & 4) == 4
     lane = lax.broadcasted_iota(jnp.int32, (16, LANES), 1)
 
-    def one_slot(slot, carry):
+    for slot in range(slots):
         left = jnp.concatenate(
             [nat_ref[g, pl.ds(slot, 16, stride=slots), :] for g in range(groups)], axis=1
         )
-        slot_copy(source_ref, table_ref, arrived, slot).wait()
         sums = lax.dot_general(
             left.astype(BF16), table_ref[slot, :FULL, :], NT, preferred_element_type=F32
         )
@@ -210,22 +206,20 @@
                 both = part[g * 8 : g * 8 + 4] + part[g * 8 + 4 : g * 8 + 8]
                 tile = jnp.concatenate([both[0:1] + both[1:2], both[2:3] + both[3:4]], axis=0)
                 out_ref[(g * slots + slot) * TILES + j] = tile.astype(BF16)
-        return carry
-
-    lax.fori_loop(0, slots, one_slot, None, unroll=2)
-
-
-def call(kernel, name, out_shape, operands, scratch=(), scalars=0, remote=0):
-    first = scalars + remote
-    spaces = [pltpu.SMEM] * scalars + [pltpu.HBM] * remote + [pltpu.VMEM] * (len(operands) - first)
+
+
+def call(kernel, name, out_shape, operands, scratch=(), scalars=0):
     operands = [
-        x if i < first else pltpu.with_memory_space_constraint(x, pltpu.VMEM)
+        x if i < scalars else pltpu.with_memory_space_constraint(x, pltpu.VMEM)
         for i, x in enumerate(operands)
     ]
     return pl.pallas_call(
         kernel,
         out_shape=tuple(pltpu.VMEM(shape, dtype) for shape, dtype in out_shape),
-        in_specs=[pl.BlockSpec(memory_space=space) for space in spaces],
+        in_specs=[
+            pl.BlockSpec(memory_space=pltpu.SMEM if i < scalars else pltpu.VMEM)
+            for i in range(len(operands))
+        ],
         out_specs=(pl.BlockSpec(memory_space=pltpu.VMEM),) * len(out_shape),
         scratch_shapes=scratch,
         compiler_params=pltpu.CompilerParams(vmem_limit_bytes=SCOPED),
@@ -269,7 +263,6 @@
     theta_row = theta_owner.reshape(1, half)
     table = trig_table(pair_slots, owners, slot_dev)
 
-    held = [pltpu.VMEM(legendre.shape, BF16), pltpu.SemaphoreType.DMA((slot_dev,))]
     flat = jnp.transpose(spectra, (0, 1, 2, 4, 3)).reshape(3 * slot_dev, 2, PACK)
     share = -(-3 * slot_dev * TILES // levels)
     (tiles,) = pl.pallas_call(
@@ -279,16 +272,30 @@
         compiler_params=pltpu.CompilerParams(vmem_limit_bytes=SCOPED),
         name="pack",
     )(flat)
-    tiles, (table, theta_row) = level_mix(tiles, synth_mat, (table, theta_row))
-
-    (outgoing,) = call(
+    tiles, (table, theta_row, where) = level_mix(tiles, synth_mat, (table, theta_row, where))
+
+    vmem = pl.BlockSpec(memory_space=pltpu.VMEM)
+    smem = pl.BlockSpec(memory_space=pltpu.SMEM)
+    outgoing, legendre = pl.pallas_call(
         synthesis_kernel,
-        "synthesis",
-        [((owners, 6 * slot_dev, LANES), BF16)],
-        (pair_slots, where, legendre, tiles, theta_row),
-        [pltpu.VMEM((groups, 24 * slot_dev, LANES), F32)] + held,
-        scalars=2,
-        remote=1,
+        out_shape=(
+            pltpu.VMEM((owners, 6 * slot_dev, LANES), BF16),
+            pltpu.VMEM(legendre.shape, BF16),
+        ),
+        in_specs=[smem, smem, pl.BlockSpec(memory_space=pltpu.HBM), vmem, vmem],
+        out_specs=(vmem, vmem),
+        scratch_shapes=[
+            pltpu.VMEM((groups, 24 * slot_dev, LANES), F32),
+            pltpu.SemaphoreType.DMA((slot_dev,)),
+        ],
+        compiler_params=pltpu.CompilerParams(vmem_limit_bytes=SYNTHESIS_SCOPED),
+        name="synthesis",
+    )(
+        pair_slots,
+        where,
+        legendre,
+        pltpu.with_memory_space_constraint(tiles, pltpu.VMEM),
+        pltpu.with_memory_space_constraint(theta_row, pltpu.VMEM),
     )
     rows = lax.all_to_all(outgoing, "ma", split_axis=0, concat_axis=0, tiled=True)
 
@@ -311,10 +318,9 @@
         analysis_kernel,
         "analysis",
         [((share * levels, 2, LANES), BF16)],
-        (pair_slots, where, legendre, returned, theta_row),
-        [pltpu.VMEM((groups, 16 * slot_dev, LANES), F32)] + held,
+        (pair_slots, where, returned, legendre, theta_row),
+        [pltpu.VMEM((groups, 16 * slot_dev, LANES), F32)],
         scalars=2,
-        remote=1,
     )
     flux = jnp.transpose(flux, (1, 0, 2))[None]
     tiles, flux = level_mix(tiles, analysis_mat, flux)

time: 160 us -> 145 us (0.906)
  blocking collectives: 68.1 us -> 84.5 us
  Pallas kernels: 26.6 us -> 14.4 us
  waiting for transfers between devices: 24.2 us -> 13.3 us
  starting transfers between devices: 25.1 us -> 19.5 us
  local copies, waits for them, and re-layouts: 11.1 us -> 7.22 us
    pallas_call x4 -> x3, Pallas kernels: 25 us -> 7.56 us  [call(): pl.pallas_call(kernel, out_shape=tuple((pltpu.VMEM(shape, dtype) for shap...]
    all_to_all x0 -> x1, blocking collectives: none -> 16.4 us  [level_mix(): lax.all_to_all(mixed, 'row', split_axis=0, concat_axis=0, tiled=True)]
    all_to_all x2 -> x1, waiting for transfers between devices: 19.1 us -> 8.22 us  [level_mix(): lax.all_to_all(mixed, 'row', split_axis=0, concat_axis=0, tiled=True)]
    all_to_all x2 -> x1, starting transfers between devices: 10.6 us -> 4.89 us  [level_mix(): lax.all_to_all(mixed, 'row', split_axis=0, concat_axis=0, tiled=True)]
    pallas_call x0 -> x1, Pallas kernels: none -> 5.3 us  [local(): pl.pallas_call(synthesis_kernel, out_shape=(pltpu.VMEM((owners, 6 * slot_...]
    unnamed x15 -> x9, local copies, waits for them, and re-layouts: 7.31 us -> 3.13 us
  transfers between devices with their start and end apart: 3 -> 2, of which waited for: 3 -> 2; matrix products, arithmetic and copies ran while one was open for 4% -> 4% of each run, Pallas kernels for 1% -> 1%
where the time goes in v2:
time: 145 us; the launch traced here: 144 us
  blocking collectives  84.5 us (58%)
  starting transfers between devices  19.5 us (13%)
  Pallas kernels  14.4 us (10%)
  waiting for transfers between devices  13.3 us (9%)
  local copies, waits for them, and re-layouts  7.22 us (5%)
  other arithmetic  2.27 us (2%)
  matrix products  2.15 us (1%)
    all_to_all x1, blocking collectives, local(): lax.all_to_all(outgoing, 'ma', split_axis=0, concat_axis=0, tiled=True)  30.8 us
    all_to_all x1, blocking collectives, level_mix(): here = lax.all_to_all(tiles, 'row', split_axis=0, concat_axis=0, tiled=True)  18.8 us
    all_to_all x1, blocking collectives, local(): lax.all_to_all(fourier, 'ma', split_axis=0, concat_axis=0, tiled=True)  18.5 us
    all_to_all x1, blocking collectives, level_mix(): lax.all_to_all(mixed, 'row', split_axis=0, concat_axis=0, tiled=True)  16.4 us
    all_to_all x1, starting transfers between devices, level_mix(): here = lax.all_to_all(tiles, 'row', split_axis=0, concat_axis=0, tiled=True)  14.6 us
    all_to_all x1, waiting for transfers between devices, level_mix(): lax.all_to_all(mixed, 'row', split_axis=0, concat_axis=0, tiled=True)  8.22 us
    pallas_call x3, Pallas kernels, call(): pl.pallas_call(kernel, out_shape=tuple((pltpu.VMEM(shape, dtype) for shap...  7.56 us
    pallas_call x1, Pallas kernels, local(): pl.pallas_call(synthesis_kernel, out_shape=(pltpu.VMEM((owners, 6 * slot_...  5.3 us
  transfers between devices with their start and end apart: 2, of which 2 were waited for; matrix products, arithmetic and copies ran while one was open for 4% of the time, Pallas kernels for 1%

profile of v2, /device:TPU:1, one launch (start us, length us, event | category | flops | bytes accessed | tf_op | source)
XLA Modules:
  0.0 144.1 jit_solution(3252645928490746531)
XLA Ops:
  0.6 0.0 copy-start.1
  0.6 1.0 copy-done.1
  1.6 0.8 pack.1
  2.4 14.6 %all-to-all-start = ((bf16[384,2,128]{2,1,0:T(2,128)(2,1)}), bf16[384,2,128]{2,1,0:T(2,128)(2,1)S(1)}, u32[]{:S(2)}, u32[]{:S(2)}) async-start(bf16[384,2,128]{2,1,0:T(2,128)(2,1)} %pack.1), calls=%async_computation | async-start | bytes 393216 | tf_op jit(solution)/shard_map/all_to_all | solution.py:233
  17.0 0.8 reshape.51
  17.8 0.7 reshape.52.theta_ref
  18.5 0.1 mul.43
  18.6 2.2 %fusion.12 = (f32[528,128]{1,0:T(8,128)S(1)}, f32[528,128]{1,0:T(8,128)S(1)}, f32[528,128]{1,0:T(8,128)S(1)}, f32[528,128]{1,0:T(8,128)S(1)}) fusion(s32[128]{0:T(128)S(1)} %iota_multiply_fusion, s32[528]{0:T(1024)S(1)} %mul.43), kind=kLoop, calls=%fused_computation.18 | loop fusion | flops 1216512 | bytes 1083968 | tf_op jit(solution)/shard_map/sin | solution.py:251
  20.9 2.0 %table.1.table_ref = bf16[1056,1536]{1,0:T(8,128)(2,1)S(1)} custom-call(f32[528,128]{1,0:T(8,128)S(1)} %get-tuple-element.25.coarse_cos_ref, f32[528,128]{1,0:T(8,128)S(1)} %get-tuple-element.24.coarse_sin_ref, f32[528,128]{1,0:T(8,128)S(1)} %get-tuple-element.27.fine_cos_ref, f32[528,128]{1,0:T(8,128)S(1)} %get-tuple-element.26.fine_sin_ref), custom_call_target="tpu_custom_call" | custom-call | tf_op jit(solution)/shard_map/table/pallas_call | solution.py:216
  22.9 0.0 copy-start.2
  22.9 5.1 %all-to-all-done = bf16[384,2,128]{2,1,0:T(2,128)(2,1)S(1)} async-done(((bf16[384,2,128]{2,1,0:T(2,128)(2,1)}), bf16[384,2,128]{2,1,0:T(2,128)(2,1)S(1)}, u32[]{:S(2)}, u32[]{:S(2)}) %all-to-all-start) | async-done | bytes 196640 | tf_op jit(solution)/shard_map/all_to_all | solution.py:233
  28.1 0.8 reshape.54
  28.8 1.9 %fusion = bf16[64,1536]{1,0:T(8,128)(2,1)} fusion(bf16[64,1536]{1,0:T(8,128)(2,1)} %reshape.54, f32[64,64]{1,0:T(8,128)} %constant.30.clone), kind=kOutput, calls=%fused_computation.1 | convolution fusion | flops 75595776 | bytes 409600 | tf_op jit(solution)/shard_map/dot_general | solution.py:236
  30.7 1.0 reshape.55
  31.7 16.4 %all_to_all.30.tiles_ref = bf16[384,2,128]{2,1,0:T(2,128)(2,1)S(1)} all-to-all(bf16[384,2,128]{2,1,0:T(2,128)(2,1)S(1)} %reshape.55), channel_id=1, replica_groups=mesh['ma'=12,'row'=64] {'row'}, dimensions={0} | all-to-all | bytes 393216 | tf_op jit(solution)/shard_map/all_to_all | solution.py:238
  48.1 5.3 %synthesis.1 = (bf16[12,132,128]{2,1,0:T(8,128)(2,1)S(1)}, bf16[22,513,384]{2,1,0:T(8,128)(2,1)S(1)}) custom-call(s32[264]{0:T(512)} %pairs_ref.3, s32[1]{0:T(128)} %bitcast.2.where_ref, bf16[22,513,384]{2,1,0:T(8,128)(2,1)} %source_ref.1, bf16[384,2,128]{2,1,0:T(2,128)(2,1)S(1)} %all_to_all.30.tiles_ref, s32[1,384]{1,0:T(1,128)S(1)} %reshape.52.theta_ref), custom_call_target="tpu_custom_call" | custom-call | tf_op jit(solution)/shard_map/synthesis/pallas_call | solution.py:279
  53.4 0.0 copy-start.3
  53.4 30.8 %all_to_all.31.rows_ref = bf16[12,132,128]{2,1,0:T(8,128)(2,1)S(1)} all-to-all(bf16[12,132,128]{2,1,0:T(8,128)(2,1)S(1)} %get-tuple-element.15), channel_id=1, replica_groups=mesh['ma'=12,'row'=64] {'ma'}, dimensions={0} | all-to-all | bytes 811008 | tf_op jit(solution)/shard_map/all_to_all | solution.py:300
  84.2 2.0 %fourier.1 = (bf16[2,64,1536]{2,1,0:T(8,128)(2,1)S(1)}, bf16[12,88,128]{2,1,0:T(8,128)(2,1)S(1)}) custom-call(bf16[12,132,128]{2,1,0:T(8,128)(2,1)S(1)} %all_to_all.31.rows_ref, bf16[1056,1536]{1,0:T(8,128)(2,1)S(1)} %table.1.table_ref), custom_call_target="tpu_custom_call" | custom-call | tf_op jit(solution)/shard_map/fourier/pallas_call | solution.py:216
  86.3 0.0 copy-start
  86.3 18.5 %all_to_all.32.rows_ref = bf16[12,88,128]{2,1,0:T(8,128)(2,1)S(1)} all-to-all(bf16[12,88,128]{2,1,0:T(8,128)(2,1)S(1)} %get-tuple-element.17), channel_id=1, replica_groups=mesh['ma'=12,'row'=64] {'ma'}, dimensions={0} | all-to-all | bytes 540672 | tf_op jit(solution)/shard_map/all_to_all | solution.py:314
  104.8 0.0 copy-done.2
  104.8 3.5 %analysis.1 = bf16[256,2,128]{2,1,0:T(2,128)(2,1)S(1)} custom-call(s32[264]{0:T(512)S(1)} %copy-done.2, s32[1]{0:T(128)} %bitcast.2.where_ref, bf16[12,88,128]{2,1,0:T(8,128)(2,1)S(1)} %all_to_all.32.rows_ref, bf16[22,513,384]{2,1,0:T(8,128)(2,1)S(1)} %get-tuple-element.18.table_ref, s32[1,384]{1,0:T(1,128)S(1)} %reshape.52.theta_ref), custom_call_target="tpu_custom_call" | custom-call | tf_op jit(solution)/shard_map/analysis/pallas_call | solution.py:216
  108.3 18.8 %all_to_all.33 = bf16[256,2,128]{2,1,0:T(2,128)(2,1)S(1)} all-to-all(bf16[256,2,128]{2,1,0:T(2,128)(2,1)S(1)} %analysis.1), channel_id=1, replica_groups=mesh['ma'=12,'row'=64] {'row'}, dimensions={0} | all-to-all | bytes 262144 | tf_op jit(solution)/shard_map/all_to_all | solution.py:233
  127.0 0.0 copy-done
  127.0 0.1 reshape.56
  127.1 0.0 copy-done.3
  127.1 0.2 fusion.1
  127.4 0.7 reshape.57
  128.1 4.9 %all-to-all-start.5 = ((bf16[256,2,128]{2,1,0:T(2,128)(2,1)}), bf16[256,2,128]{2,1,0:T(2,128)(2,1)S(1)}, u32[]{:S(2)}, u32[]{:S(2)}) async-start(bf16[256,2,128]{2,1,0:T(2,128)(2,1)} %reshape.57), calls=%async_computation.5 | async-start | bytes 262144 | tf_op jit(solution)/shard_map/all_to_all | solution.py:238
  133.0 2.1 %copy.8 = bf16[1,64,2,1536]{3,2,1,0:T(2,128)(2,1)} copy(bf16[1,64,2,1536]{3,1,2,0:T(8,128)(2,1)} %bitcast.18) | data formatting | bytes 786432
  135.2 8.2 %all-to-all-done.5.tiles_ref = bf16[256,2,128]{2,1,0:T(2,128)(2,1)S(1)} async-done(((bf16[256,2,128]{2,1,0:T(2,128)(2,1)}), bf16[256,2,128]{2,1,0:T(2,128)(2,1)S(1)}, u32[]{:S(2)}, u32[]{:S(2)}) %all-to-all-start.5) | async-done | bytes 131104 | tf_op jit(solution)/shard_map/all_to_all | solution.py:238
  143.4 0.8 unpack.1
  (3 shorter events, 0.0 us)
Async XLA Ops:
  0.6 1.0 copy-start.1
  2.4 25.6 %all-to-all-start = ((bf16[384,2,128]{2,1,0:T(2,128)(2,1)}), bf16[384,2,128]{2,1,0:T(2,128)(2,1)S(1)}, u32[]{:S(2)}, u32[]{:S(2)}) async-start(bf16[384,2,128]{2,1,0:T(2,128)(2,1)} %pack.1), calls=%async_computation | async-start | bytes 393216 | tf_op jit(solution)/shard_map/all_to_all | solution.py:233
  22.9 81.8 %copy-start.2 = (s32[264]{0:T(512)S(1)}, s32[264]{0:T(512)}, u32[]{:S(2)}) copy-start(s32[264]{0:T(512)} %pairs_ref.3) | copy-start | bytes 3172
  53.4 73.7 %copy-start.3 = (f32[64,64]{1,0:T(8,128)S(1)}, f32[64,64]{1,0:T(8,128)}, u32[]{:S(2)}) copy-start(f32[64,64]{1,0:T(8,128)} %constant.31.clone) | copy-start | bytes 49156
  86.3 40.8 %copy-start = (bf16[2,64,1536]{2,1,0:T(8,128)(2,1)}, bf16[2,64,1536]{2,1,0:T(8,128)(2,1)S(1)}, u32[]{:S(2)}) copy-start(bf16[2,64,1536]{2,1,0:T(8,128)(2,1)S(1)} %get-tuple-element.19) | copy-start | bytes 1179652
  128.1 15.3 %all-to-all-start.5 = ((bf16[256,2,128]{2,1,0:T(2,128)(2,1)}), bf16[256,2,128]{2,1,0:T(2,128)(2,1)S(1)}, u32[]{:S(2)}, u32[]{:S(2)}) async-start(bf16[256,2,128]{2,1,0:T(2,128)(2,1)} %reshape.57), calls=%async_computation.5 | async-start | bytes 262144 | tf_op jit(solution)/shard_map/all_to_all | solution.py:238

commit v3 on v2

--- a/solution.py
+++ b/solution.py
@@ -21,7 +21,6 @@
 GROUP = 4
 BF16 = jnp.bfloat16
 F32 = jnp.float32
-HIGH = lax.Precision.HIGHEST
 NT = (((1,), (1,)), ((), ()))
 
 
@@ -41,13 +40,16 @@
 
 def pack_kernel(spectra_ref, out_ref):
     pairs = spectra_ref.shape[0]
+    whole = PACK // LANES
     lane = lax.broadcasted_iota(jnp.int32, (2, LANES), 1)
+    last = jnp.zeros((2, LANES), F32)
     for i in range(pairs):
-        for j in range(TILES - 1):
-            out_ref[i * TILES + j] = spectra_ref[i, :, j * LANES : (j + 1) * LANES].astype(BF16)
-        last = jnp.broadcast_to(spectra_ref[i, :, FULL:PACK], (2, LANES))
-        out_ref[i * TILES + TILES - 1] = jnp.where(lane == 0, last, 0.0).astype(BF16)
-    for t in range(pairs * TILES, out_ref.shape[0]):
+        for j in range(whole):
+            out_ref[i * whole + j] = spectra_ref[i, :, j * LANES : (j + 1) * LANES].astype(BF16)
+        value = jnp.broadcast_to(spectra_ref[i, :, FULL:PACK], (2, LANES))
+        last = jnp.where(lane == i, value, last)
+    out_ref[pairs * whole] = last.astype(BF16)
+    for t in range(pairs * whole + 1, out_ref.shape[0]):
         out_ref[t] = jnp.zeros((2, LANES), BF16)
 
 
@@ -85,6 +87,7 @@
     odd = (row & 1) == 1
     field = row >> 1
     lane = lax.broadcasted_iota(jnp.int32, (8, LANES), 1)
+    last = tiles_ref[3 * slots * (TILES - 1)].astype(F32)
 
     for slot in range(slots):
         if (slot - 2) % GROUP == 0 or slot == 0:
@@ -94,7 +97,15 @@
         weight = jnp.where((pair == 0) & (row & 1 == 0), 1.0, 2.0)
         blocks = [[], [], [], []]
         for j in range(TILES):
-            tiles = [tiles_ref[(f * slots + slot) * TILES + j].astype(F32) for f in range(3)]
+            if j < TILES - 1:
+                tiles = [
+                    tiles_ref[(f * slots + slot) * (TILES - 1) + j].astype(F32) for f in range(3)
+                ]
+            else:
+                tiles = [
+                    jnp.broadcast_to(last[:, f * slots + slot : f * slots + slot + 1], (2, LANES))
+                    for f in range(3)
+                ]
             mask, sign = slot_masks(pair, lane + j * LANES, odd)
             mask = mask * weight
             for c in range(2):
@@ -126,7 +137,10 @@
         ).astype(BF16)
 
 
-def table_kernel(coarse_cos_ref, coarse_sin_ref, fine_cos_ref, fine_sin_ref, out_ref):
+def table_kernel(
+    coarse_cos_ref, coarse_sin_ref, fine_cos_ref, fine_sin_ref, matrix_ref, out_ref, kept_ref
+):
+    kept_ref[...] = matrix_ref[...]
     rows = fine_cos_ref.shape[0]
     fine_cos = fine_cos_ref[...]
     fine_sin = fine_sin_ref[...]
@@ -227,18 +241,43 @@
     )(*operands)
 
 
-def level_mix(tiles, matrix, beside=None):
-    levels = matrix.shape[0]
-    share = tiles.shape[0] // levels
+def mix_kernel(tiles_ref, matrix_ref, out_ref, wide_ref):
+    levels = matrix_ref.shape[0]
+    count = tiles_ref.shape[0]
+    rows = 2 * count // levels
+    for t in range(count):
+        wide_ref[2 * t : 2 * t + 2, :] = tiles_ref[t].astype(F32)
+    right = jnp.concatenate(
+        [wide_ref[pl.ds(i, levels, stride=rows), :] for i in range(rows)], axis=1
+    ).astype(BF16)
+    right = jnp.concatenate([right, right], axis=0)
+    mixed = jnp.dot(matrix_ref[...], right, preferred_element_type=F32)
+    for i in range(rows):
+        wide_ref[pl.ds(i, levels, stride=rows), :] = mixed[:, i * LANES : (i + 1) * LANES]
+    for t in range(count):
+        out_ref[t] = wide_ref[2 * t : 2 * t + 2, :].astype(BF16)
+
+
+def two_parts(matrix):
+    upper = jnp.asarray(matrix).astype(BF16)
+    lower = (matrix - upper.astype(F32)).astype(BF16)
+    return jnp.concatenate([upper, lower], axis=1)
+
+
+def level_mix(tiles, parts, beside=None):
     here = lax.all_to_all(tiles, "row", split_axis=0, concat_axis=0, tiled=True)
-    here, beside = lax.optimization_barrier((here, beside))
-    here = here.reshape(levels, share * 2 * LANES).astype(F32)
-    mixed = jnp.dot(matrix, here, precision=HIGH).astype(BF16)
-    mixed = mixed.reshape(levels * share, 2, LANES)
+    here, beside, parts = lax.optimization_barrier((here, beside, parts))
+    (mixed,) = call(
+        mix_kernel,
+        "mix",
+        [(tiles.shape, BF16)],
+        (here, parts),
+        [pltpu.VMEM((2 * tiles.shape[0], LANES), F32)],
+    )
     return lax.all_to_all(mixed, "row", split_axis=0, concat_axis=0, tiled=True), beside
 
 
-def trig_table(pair_slots, owners, slot_dev):
+def trig_table(pair_slots, owners, slot_dev, parts):
     pairs = pair_slots.reshape(owners, 1, slot_dev)
     orders = jnp.concatenate([pairs, LMAX - pairs], axis=1).reshape(-1, 1)
     span = lax.broadcasted_iota(jnp.int32, (1, LANES), 1)
@@ -249,7 +288,7 @@
     fine = fine.astype(F32) * scale
     shape = (2 * orders.shape[0], NPHI)
     trig = (jnp.cos(coarse), jnp.sin(coarse), jnp.cos(fine), jnp.sin(fine))
-    return call(table_kernel, "table", [(shape, BF16)], trig)[0]
+    return call(table_kernel, "table", [(shape, BF16), (parts.shape, BF16)], trig + (parts,))
 
 
 def local(spectra, legendre, pair_slots, theta_owner):
@@ -261,10 +300,10 @@
     synth_mat, analysis_mat = chebyshev_pair(levels)
     where = lax.axis_index("ma").astype(jnp.int32).reshape(1)
     theta_row = theta_owner.reshape(1, half)
-    table = trig_table(pair_slots, owners, slot_dev)
+    table, synth_parts = trig_table(pair_slots, owners, slot_dev, two_parts(synth_mat))
 
     flat = jnp.transpose(spectra, (0, 1, 2, 4, 3)).reshape(3 * slot_dev, 2, PACK)
-    share = -(-3 * slot_dev * TILES // levels)
+    share = -(-(3 * slot_dev * (TILES - 1) + 1) // levels)
     (tiles,) = pl.pallas_call(
         pack_kernel,
         out_shape=(pltpu.VMEM((share * levels, 2, LANES), BF16),),
@@ -272,7 +311,7 @@
         compiler_params=pltpu.CompilerParams(vmem_limit_bytes=SCOPED),
         name="pack",
     )(flat)
-    tiles, (table, theta_row, where) = level_mix(tiles, synth_mat, (table, theta_row, where))
+    tiles, (table, theta_row, where) = level_mix(tiles, synth_parts, (table, theta_row, where))
 
     vmem = pl.BlockSpec(memory_space=pltpu.VMEM)
     smem = pl.BlockSpec(memory_space=pltpu.SMEM)
@@ -323,7 +362,7 @@
         scalars=2,
     )
     flux = jnp.transpose(flux, (1, 0, 2))[None]
-    tiles, flux = level_mix(tiles, analysis_mat, flux)
+    tiles, flux = level_mix(tiles, two_parts(analysis_mat), flux)
     tiles = pltpu.with_memory_space_constraint(tiles, pltpu.VMEM)
     result = pl.pallas_call(
         unpack_kernel,

time: 145 us -> 141 us (0.972)
  matrix products: 2.15 us -> 0 us
  local copies, waits for them, and re-layouts: 7.22 us -> 5.4 us
    reshape x4 -> x0, local copies, waits for them, and re-layouts: 2.53 us -> none  [the longest x2 1.7 us: level_mix(): mixed = mixed.reshape(levels * share, 2, LANES)]
    dot_general x2 -> x0, matrix products: 2.15 us -> none  [level_mix(): mixed = jnp.dot(matrix, here, precision=HIGH).astype(BF16)]
    pallas_call x3 -> x5, Pallas kernels: 7.56 us -> 8.89 us  [call(): pl.pallas_call(kernel, out_shape=tuple((pltpu.VMEM(shape, dtype) for shap...]
    unnamed x9 -> x11, local copies, waits for them, and re-layouts: 3.13 us -> 3.84 us
where the time goes in v3:
time: 141 us; the launch traced here: 140 us
  blocking collectives  84.5 us (60%)
  starting transfers between devices  19.4 us (14%)
  Pallas kernels  15.8 us (11%)
  waiting for transfers between devices  12.3 us (9%)
  local copies, waits for them, and re-layouts  5.4 us (4%)
  other arithmetic  2.27 us (2%)
    all_to_all x1, blocking collectives, local(): lax.all_to_all(outgoing, 'ma', split_axis=0, concat_axis=0, tiled=True)  30.8 us
    all_to_all x1, blocking collectives, local(): lax.all_to_all(fourier, 'ma', split_axis=0, concat_axis=0, tiled=True)  18.5 us
    all_to_all x1, blocking collectives, level_mix(): here = lax.all_to_all(tiles, 'row', split_axis=0, concat_axis=0, tiled=True)  18.4 us
    all_to_all x1, blocking collectives, level_mix(): lax.all_to_all(mixed, 'row', split_axis=0, concat_axis=0, tiled=True)  16.8 us
    all_to_all x1, starting transfers between devices, level_mix(): here = lax.all_to_all(tiles, 'row', split_axis=0, concat_axis=0, tiled=True)  14.6 us
    pallas_call x5, Pallas kernels, call(): pl.pallas_call(kernel, out_shape=tuple((pltpu.VMEM(shape, dtype) for shap...  8.89 us
    all_to_all x1, waiting for transfers between devices, level_mix(): lax.all_to_all(mixed, 'row', split_axis=0, concat_axis=0, tiled=True)  8.22 us
    pallas_call x1, Pallas kernels, local(): pl.pallas_call(synthesis_kernel, out_shape=(pltpu.VMEM((owners, 6 * slot_...  5.32 us
  transfers between devices with their start and end apart: 2, of which 2 were waited for; matrix products, arithmetic and copies ran while one was open for 4% of the time, Pallas kernels for 1%

profile of v3, /device:TPU:1, one launch (start us, length us, event | category | flops | bytes accessed | tf_op | source)
XLA Modules:
  0.0 140.4 jit_solution(9281517449348675029)
XLA Ops:
  0.6 0.0 copy-start.1
  0.6 1.0 copy-done.1
  1.6 0.0 copy-start.2
  1.6 0.8 pack.1
  2.4 14.6 %all-to-all-start = ((bf16[320,2,128]{2,1,0:T(2,128)(2,1)}), bf16[320,2,128]{2,1,0:T(2,128)(2,1)S(1)}, u32[]{:S(2)}, u32[]{:S(2)}) async-start(bf16[320,2,128]{2,1,0:T(2,128)(2,1)} %pack.1), calls=%async_computation | async-start | bytes 327680 | tf_op jit(solution)/shard_map/all_to_all | solution.py:268
  17.0 0.7 reshape.40.theta_ref
  17.7 0.8 reshape.39
  18.5 0.1 mul.43
  18.6 2.2 %fusion.10 = (f32[528,128]{1,0:T(8,128)S(1)}, f32[528,128]{1,0:T(8,128)S(1)}, f32[528,128]{1,0:T(8,128)S(1)}, f32[528,128]{1,0:T(8,128)S(1)}) fusion(s32[128]{0:T(128)S(1)} %iota_multiply_fusion, s32[528]{0:T(1024)S(1)} %mul.43), kind=kLoop, calls=%fused_computation.14 | loop fusion | flops 1216512 | bytes 1083968 | tf_op jit(solution)/shard_map/sin | solution.py:290
  20.9 0.0 copy-start.3
  20.9 0.7 copy-done.3
  21.6 2.0 %table.1 = (bf16[1056,1536]{1,0:T(8,128)(2,1)S(1)}, bf16[64,128]{1,0:T(8,128)(2,1)S(1)}) custom-call(f32[528,128]{1,0:T(8,128)S(1)} %get-tuple-element.33.coarse_cos_ref, f32[528,128]{1,0:T(8,128)S(1)} %get-tuple-element.32.coarse_sin_ref, f32[528,128]{1,0:T(8,128)S(1)} %get-tuple-element.35.fine_cos_ref, f32[528,128]{1,0:T(8,128)S(1)} %get-tuple-element.34.fine_sin_ref, ...), custom_call_target="tpu_custom_call" | custom-call | tf_op jit(solution)/shard_map/table/pallas_call | solution.py:230
  23.6 4.1 %all-to-all-done.tiles_ref = bf16[320,2,128]{2,1,0:T(2,128)(2,1)S(1)} async-done(((bf16[320,2,128]{2,1,0:T(2,128)(2,1)}), bf16[320,2,128]{2,1,0:T(2,128)(2,1)S(1)}, u32[]{:S(2)}, u32[]{:S(2)}) %all-to-all-start) | async-done | bytes 163872 | tf_op jit(solution)/shard_map/all_to_all | solution.py:268
  27.7 0.3 mix.2
  28.0 16.8 %all_to_all.30.tiles_ref = bf16[320,2,128]{2,1,0:T(2,128)(2,1)S(1)} all-to-all(bf16[320,2,128]{2,1,0:T(2,128)(2,1)S(1)} %mix.2), channel_id=1, replica_groups=mesh['ma'=12,'row'=64] {'row'}, dimensions={0} | all-to-all | bytes 327680 | tf_op jit(solution)/shard_map/all_to_all | solution.py:277
  44.8 5.3 %synthesis.1 = (bf16[12,132,128]{2,1,0:T(8,128)(2,1)S(1)}, bf16[22,513,384]{2,1,0:T(8,128)(2,1)S(1)}) custom-call(s32[264]{0:T(512)} %pairs_ref.3, s32[1]{0:T(128)} %bitcast.2.where_ref, bf16[22,513,384]{2,1,0:T(8,128)(2,1)} %source_ref.1, bf16[320,2,128]{2,1,0:T(2,128)(2,1)S(1)} %all_to_all.30.tiles_ref, s32[1,384]{1,0:T(1,128)S(1)} %reshape.40.theta_ref), custom_call_target="tpu_custom_call" | custom-call | tf_op jit(solution)/shard_map/synthesis/pallas_call | solution.py:318
  50.1 0.0 copy-start.4
  50.1 30.8 %all_to_all.31.rows_ref = bf16[12,132,128]{2,1,0:T(8,128)(2,1)S(1)} all-to-all(bf16[12,132,128]{2,1,0:T(8,128)(2,1)S(1)} %get-tuple-element.22), channel_id=1, replica_groups=mesh['ma'=12,'row'=64] {'ma'}, dimensions={0} | all-to-all | bytes 811008 | tf_op jit(solution)/shard_map/all_to_all | solution.py:339
  80.9 2.0 %fourier.1 = (bf16[2,64,1536]{2,1,0:T(8,128)(2,1)S(1)}, bf16[12,88,128]{2,1,0:T(8,128)(2,1)S(1)}) custom-call(bf16[12,132,128]{2,1,0:T(8,128)(2,1)S(1)} %all_to_all.31.rows_ref, bf16[1056,1536]{1,0:T(8,128)(2,1)S(1)} %get-tuple-element.23.table_ref), custom_call_target="tpu_custom_call" | custom-call | tf_op jit(solution)/shard_map/fourier/pallas_call | solution.py:230
  83.0 0.0 copy-start
  83.0 18.5 %all_to_all.32.rows_ref = bf16[12,88,128]{2,1,0:T(8,128)(2,1)S(1)} all-to-all(bf16[12,88,128]{2,1,0:T(8,128)(2,1)S(1)} %get-tuple-element.24), channel_id=1, replica_groups=mesh['ma'=12,'row'=64] {'ma'}, dimensions={0} | all-to-all | bytes 540672 | tf_op jit(solution)/shard_map/all_to_all | solution.py:353
  101.5 0.0 copy-done.2
  101.5 3.5 %analysis.1 = bf16[256,2,128]{2,1,0:T(2,128)(2,1)S(1)} custom-call(s32[264]{0:T(512)S(1)} %copy-done.2, s32[1]{0:T(128)} %bitcast.2.where_ref, bf16[12,88,128]{2,1,0:T(8,128)(2,1)S(1)} %all_to_all.32.rows_ref, bf16[22,513,384]{2,1,0:T(8,128)(2,1)S(1)} %get-tuple-element.25.table_ref, s32[1,384]{1,0:T(1,128)S(1)} %reshape.40.theta_ref), custom_call_target="tpu_custom_call" | custom-call | tf_op jit(solution)/shard_map/analysis/pallas_call | solution.py:230
  105.0 18.4 %all_to_all.33.tiles_ref = bf16[256,2,128]{2,1,0:T(2,128)(2,1)S(1)} all-to-all(bf16[256,2,128]{2,1,0:T(2,128)(2,1)S(1)} %analysis.1), channel_id=1, replica_groups=mesh['ma'=12,'row'=64] {'row'}, dimensions={0} | all-to-all | bytes 262144 | tf_op jit(solution)/shard_map/all_to_all | solution.py:268
  123.4 0.0 copy-done
  123.4 0.0 copy-done.4
  123.4 1.0 mix.3
  124.4 4.9 %all-to-all-start.5 = ((bf16[256,2,128]{2,1,0:T(2,128)(2,1)}), bf16[256,2,128]{2,1,0:T(2,128)(2,1)S(1)}, u32[]{:S(2)}, u32[]{:S(2)}) async-start(bf16[256,2,128]{2,1,0:T(2,128)(2,1)} %mix.3), calls=%async_computation.5 | async-start | bytes 262144 | tf_op jit(solution)/shard_map/all_to_all | solution.py:277
  129.3 2.1 %copy.8 = bf16[1,64,2,1536]{3,2,1,0:T(2,128)(2,1)} copy(bf16[1,64,2,1536]{3,1,2,0:T(8,128)(2,1)} %bitcast.10) | data formatting | bytes 786432
  131.4 8.2 %all-to-all-done.5.tiles_ref = bf16[256,2,128]{2,1,0:T(2,128)(2,1)S(1)} async-done(((bf16[256,2,128]{2,1,0:T(2,128)(2,1)}), bf16[256,2,128]{2,1,0:T(2,128)(2,1)S(1)}, u32[]{:S(2)}, u32[]{:S(2)}) %all-to-all-start.5) | async-done | bytes 131104 | tf_op jit(solution)/shard_map/all_to_all | solution.py:277
  139.6 0.8 unpack.1
  (3 shorter events, 0.0 us)
Async XLA Ops:
  0.6 1.0 copy-start.1
  1.6 99.9 %copy-start.2 = (s32[264]{0:T(512)S(1)}, s32[264]{0:T(512)}, u32[]{:S(2)}) copy-start(s32[264]{0:T(512)} %pairs_ref.3) | copy-start | bytes 3172
  2.4 25.3 %all-to-all-start = ((bf16[320,2,128]{2,1,0:T(2,128)(2,1)}), bf16[320,2,128]{2,1,0:T(2,128)(2,1)S(1)}, u32[]{:S(2)}, u32[]{:S(2)}) async-start(bf16[320,2,128]{2,1,0:T(2,128)(2,1)} %pack.1), calls=%async_computation | async-start | bytes 327680 | tf_op jit(solution)/shard_map/all_to_all | solution.py:268
  20.9 0.7 copy-start.3
  50.1 73.3 %copy-start.4 = (bf16[64,128]{1,0:T(8,128)(2,1)S(1)}, bf16[64,128]{1,0:T(8,128)(2,1)}, u32[]{:S(2)}) copy-start(bf16[64,128]{1,0:T(8,128)(2,1)} %constant.43.matrix_ref) | copy-start | bytes 49156
  83.0 40.4 %copy-start = (bf16[2,64,1536]{2,1,0:T(8,128)(2,1)}, bf16[2,64,1536]{2,1,0:T(8,128)(2,1)S(1)}, u32[]{:S(2)}) copy-start(bf16[2,64,1536]{2,1,0:T(8,128)(2,1)S(1)} %get-tuple-element.26) | copy-start | bytes 1179652
  124.4 15.2 %all-to-all-start.5 = ((bf16[256,2,128]{2,1,0:T(2,128)(2,1)}), bf16[256,2,128]{2,1,0:T(2,128)(2,1)S(1)}, u32[]{:S(2)}, u32[]{:S(2)}) async-start(bf16[256,2,128]{2,1,0:T(2,128)(2,1)} %mix.3), calls=%async_computation.5 | async-start | bytes 262144 | tf_op jit(solution)/shard_map/all_to_all | solution.py:277

commit v4 on v2

v4 whole, which is shorter than its diff:
```python
import math

import jax
import jax.numpy as jnp
import numpy as np
from jax import lax
from jax.experimental import pallas as pl
from jax.experimental.pallas import tpu as pltpu
from jax.sharding import PartitionSpec as P

LMAX = 511
NPHI = 1536
NPAIRS = 256
PACK = 513
LANES = 128
TILES = -(-PACK // LANES)
FULL = PACK // LANES * LANES
WIDTH = 256
SCOPED = 16 << 20
LEGENDRE_SCOPED = 56 << 20
GROUP = 4
BF16 = jnp.bfloat16
F32 = jnp.float32
NT = (((1,), (1,)), ((), ()))


def chebyshev_pair(levels):
    index = np.arange(levels)
    cosines = np.cos(np.pi * (np.outer(index, index) % (2 * (levels - 1))) / (levels - 1))
    ends = np.where((index == 0) | (index == levels - 1), 0.5, 1.0)
    analysis = (2.0 / (levels - 1)) ** 0.5 * np.outer(ends, ends) * cosines
    return cosines.astype(np.float32), analysis.astype(np.float32)


def one_hot(theta_row):
    half = theta_row.shape[1]
    natural = lax.broadcasted_iota(jnp.int32, (half, half), 0)
    return jnp.where(natural == theta_row, 1.0, 0.0).astype(BF16)


def slot_masks(pair, column, order_odd):
    used = pair < NPAIRS
    low = jnp.where(used & (column <= LMAX - pair), 1.0, 0.0)
    high = jnp.where(used & (column > LMAX - pair), 1.0, 0.0)
    low_sign = (1 - 2 * (column & 1)).astype(F32)
    high_sign = (1 - 2 * ((column + pair) & 1)).astype(F32)
    return jnp.where(order_odd, high, low), jnp.where(order_odd, high_sign, low_sign)


def start_copies(source_ref, table_ref, arrived):
    copies = [
        pltpu.make_async_copy(source_ref.at[slot], table_ref.at[slot], arrived.at[slot])
        for slot in range(table_ref.shape[0])
    ]
    for copy in copies:
        copy.start()
    return copies


def wait_group(copies, slot):
    if slot == 0 or (slot - 2) % GROUP == 0:
        for copy in copies[slot : slot + GROUP if slot else 2]:
            copy.wait()


def synthesis_kernel(
    pairs_ref, source_ref, spectra_ref, theta_ref, out_ref, rows_ref, table_ref, arrived
):
    slots = table_ref.shape[0]
    copies = start_copies(source_ref, table_ref, arrived)
    first = lax.axis_index("ma") * slots
    owners = out_ref.shape[0]
    own_half = theta_ref.shape[1] // owners
    groups = rows_ref.shape[0]
    block = 6 * slots
    row = lax.broadcasted_iota(jnp.int32, (8, LANES), 0)
    odd = (row & 1) == 1
    field = row >> 1
    lane = lax.broadcasted_iota(jnp.int32, (8, LANES), 1)

    for slot in range(slots):
        wait_group(copies, slot)
        pair = pairs_ref[first + slot]
        weight = jnp.where((pair == 0) & (row & 1 == 0), 1.0, 2.0)
        blocks = [[], [], [], []]
        for j in range(TILES):
            picked = [f * slots + slot for f in range(3)]
            if j < TILES - 1:
                tiles = [spectra_ref[i, :, j * LANES : (j + 1) * LANES] for i in picked]
            else:
                tiles = [
                    jnp.broadcast_to(spectra_ref[i, :, FULL:PACK], (2, LANES)) for i in picked
                ]
            mask, sign = slot_masks(pair, lane + j * LANES, odd)
            mask = mask * weight
            for c in range(2):
                parts = [jnp.broadcast_to(t[c : c + 1], (8, LANES)) for t in tiles]
                base = jnp.where(field == 0, parts[0], jnp.where(field == 1, parts[1], parts[2]))
                base = base * mask
                blocks[2 * c].append(base)
                blocks[2 * c + 1].append(base * sign)
        left = jnp.concatenate([jnp.concatenate(b, axis=1) for b in blocks], axis=0)
        sums = jnp.dot(
            left[:, :FULL].astype(BF16), table_ref[slot, :FULL, :], preferred_element_type=F32
        )
        sums = sums + left[:, FULL : FULL + 1] * table_ref[slot, FULL:PACK, :].astype(F32)
        for k in range(4):
            for g in range(groups):
                rows_ref[g, pl.ds(k * block + slot, 6, stride=slots), :] = sums[
                    k * 8 : k * 8 + 6, g * LANES : (g + 1) * LANES
                ]
    select = one_hot(theta_ref[...])
    moved = []
    for k in range(4):
        rows = jnp.concatenate(
            [rows_ref[g, k * block : (k + 1) * block, :] for g in range(groups)], axis=1
        ).astype(BF16)
        moved.append(jnp.dot(rows, select, preferred_element_type=F32))
    for d in range(owners):
        out_ref[d] = jnp.concatenate(
            [m[:, d * own_half : (d + 1) * own_half] for m in moved], axis=1
        ).astype(BF16)


def table_kernel(
    coarse_cos_ref, coarse_sin_ref, fine_cos_ref, fine_sin_ref, synth_ref, analysis_ref,
    out_ref, kept_synth_ref, kept_analysis_ref,
):
    kept_synth_ref[...] = synth_ref[...]
    kept_analysis_ref[...] = analysis_ref[...]
    rows = fine_cos_ref.shape[0]
    fine_cos = fine_cos_ref[...]
    fine_sin = fine_sin_ref[...]
    for a in range(NPHI // LANES):
        cos_a = coarse_cos_ref[:, a : a + 1]
        sin_a = coarse_sin_ref[:, a : a + 1]
        span = slice(a * LANES, (a + 1) * LANES)
        out_ref[:rows, span] = (cos_a * fine_cos - sin_a * fine_sin).astype(BF16)
        out_ref[rows:, span] = (-(sin_a * fine_cos + cos_a * fine_sin)).astype(BF16)


def scatter_row(wide_ref, row, rows, value):
    wide_ref[pl.ds(row, value.shape[0], stride=rows), :] = value


def scatter_rows(wide_ref, row, rows, values):
    full = values[0].shape[1] // LANES
    for value in values:
        for j in range(full):
            scatter_row(wide_ref, row, rows, value[:, j * LANES : (j + 1) * LANES])
            row += 1
    rest = [value[:, full * LANES :] for value in values]
    filled = sum(r.shape[1] for r in rest)
    rest.append(jnp.zeros((rest[0].shape[0], LANES - filled), F32))
    scatter_row(wide_ref, row, rows, jnp.concatenate(rest, axis=1))
    scatter_row(wide_ref, row + 1, rows, jnp.zeros_like(values[0][:, :LANES]))


def gather_rows(wide_ref, count, rows, arrays, width):
    full = width // LANES
    line = lambda row: wide_ref[pl.ds(row, count, stride=rows), :]
    rest = line(arrays * full)
    part = width - full * LANES
    return [
        jnp.concatenate(
            [line(a * full + j) for j in range(full)] + [rest[:, a * part : (a + 1) * part]],
            axis=1,
        )
        for a in range(arrays)
    ]


def widen(tiles_ref, wide_ref, count, stride, taken):
    for i in range(count):
        for t in range(taken):
            line = 2 * (i * taken + t)
            wide_ref[line : line + 2, :] = tiles_ref[i * stride + t].astype(F32)


def narrow(wide_ref, tiles_ref):
    for t in range(tiles_ref.shape[0]):
        tiles_ref[t] = wide_ref[2 * t : 2 * t + 2, :].astype(BF16)


def turn_kernel(rows_ref, out_ref, wide_ref):
    owners = rows_ref.shape[0]
    part = rows_ref.shape[1] // 3
    theta = rows_ref.shape[2] // 2
    wide = [rows_ref[d].astype(F32) for d in range(owners)]
    lines = []
    for f in range(3):
        turned = jnp.concatenate([w[f * part : (f + 1) * part] for w in wide], axis=0).T
        lines.append(jnp.concatenate([turned[:theta], turned[theta:]], axis=1))
    scatter_rows(wide_ref, 0, wide_ref.shape[0] // theta, lines)
    narrow(wide_ref, out_ref)


def grid_kernel(
    tiles_ref, table_ref, synth_ref, analysis_ref, out_ref, wide_ref, left_ref, both_ref, out_wide_ref
):
    levels = synth_ref.shape[0]
    orders = table_ref.shape[0]
    per_level = tiles_ref.shape[0] // levels
    widen(tiles_ref, wide_ref, levels, per_level, per_level)
    for f, line in enumerate(gather_rows(wide_ref, levels, 2 * per_level, 3, orders)):
        line = line.astype(BF16)
        left_ref[f * levels : (f + 1) * levels, :] = jnp.dot(
            synth_ref[...], jnp.concatenate([line, line], axis=0), preferred_element_type=F32
        ).astype(BF16)
    rows = out_wide_ref.shape[0] // levels
    flux_row = rows - 2 * NPHI // LANES
    for q in range(NPHI // WIDTH):
        span = slice(q * WIDTH, (q + 1) * WIDTH)
        grid = jnp.dot(left_ref[...], table_ref[:, span], preferred_element_type=F32)
        for g in range(2):
            flux = (grid[:levels] * grid[(1 + g) * levels : (2 + g) * levels]).astype(BF16)
            both_ref[g * levels : (g + 1) * levels, span] = flux
            flux = flux.astype(F32)
            for j in range(WIDTH // LANES):
                row = flux_row + 2 * (q * (WIDTH // LANES) + j) + g
                scatter_row(out_wide_ref, row, rows, flux[:, j * LANES : (j + 1) * LANES])
    fourier = lax.dot_general(
        both_ref[...], table_ref[...], NT, preferred_element_type=F32
    ) * NPHI ** (-0.5)
    mixed = []
    for g in range(2):
        value = fourier[g * levels : (g + 1) * levels]
        upper = value.astype(BF16)
        lower = (value - upper.astype(F32)).astype(BF16)
        right = jnp.concatenate([upper, lower, upper], axis=0)
        mixed.append(jnp.dot(analysis_ref[...], right, preferred_element_type=F32))
    scatter_rows(out_wide_ref, 0, rows, mixed)
    narrow(out_wide_ref, out_ref)


def return_kernel(tiles_ref, out_ref, wide_ref, sum_ref):
    owners = out_ref.shape[0]
    part = out_ref.shape[1] // 2
    orders = 2 * owners * part
    theta = out_ref.shape[2] // 2
    taken = wide_ref.shape[0] // (2 * theta)
    widen(tiles_ref, wide_ref, theta, tiles_ref.shape[0] // theta, taken)
    lines = gather_rows(wide_ref, theta, 2 * taken, 2, orders)
    sum_ref[...] = jnp.concatenate(lines, axis=0).T
    for d in range(owners):
        out_ref[d] = jnp.concatenate(
            [
                sum_ref[c * owners * part + d * part : c * owners * part + (d + 1) * part, :]
                for c in range(2)
            ],
            axis=0,
        ).astype(BF16)


def flux_kernel(tiles_ref, out_ref):
    theta = out_ref.shape[0]
    stride = tiles_ref.shape[0] // theta
    count = NPHI // LANES
    for t in range(theta):
        for q in range(count):
            out_ref[t, :, q * LANES : (q + 1) * LANES] = tiles_ref[t * stride + stride - count + q]


def analysis_kernel(
    pairs_ref, source_ref, rows_ref, theta_ref, out_ref, nat_ref, table_ref, arrived
):
    slots = table_ref.shape[0]
    copies = start_copies(source_ref, table_ref, arrived)
    first = lax.axis_index("ma") * slots
    owners = rows_ref.shape[0]
    own_half = theta_ref.shape[1] // owners
    block = rows_ref.shape[1]
    groups = nat_ref.shape[0]
    select = one_hot(theta_ref[...])
    wide = [rows_ref[d].astype(F32) for d in range(owners)]
    for k in range(4):
        own = jnp.concatenate([w[:, k * own_half : (k + 1) * own_half] for w in wide], axis=1)
        nat = lax.dot_general(own.astype(BF16), select, NT, preferred_element_type=F32)
        for g in range(groups):
            nat_ref[g, k * block : (k + 1) * block, :] = nat[:, g * LANES : (g + 1) * LANES]
    row = lax.broadcasted_iota(jnp.int32, (16, LANES), 0)
    odd = (row & 1) == 1
    south = (row & 4) == 4
    lane = lax.broadcasted_iota(jnp.int32, (16, LANES), 1)

    for slot in range(slots):
        left = jnp.concatenate(
            [nat_ref[g, pl.ds(slot, 16, stride=slots), :] for g in range(groups)], axis=1
        )
        wait_group(copies, slot)
        sums = lax.dot_general(
            left.astype(BF16), table_ref[slot, :FULL, :], NT, preferred_element_type=F32
        )
        last = jnp.sum(left * table_ref[slot, FULL:PACK, :].astype(F32), axis=1, keepdims=True)
        pair = pairs_ref[first + slot]
        for j in range(TILES):
            mask, sign = slot_masks(pair, lane + j * LANES, odd)
            if j < TILES - 1:
                part = sums[:, j * LANES : (j + 1) * LANES]
            else:
                part = jnp.where(lane == 0, last, 0.0)
            part = part * mask * jnp.where(south, sign, 1.0)
            for g in range(2):
                both = part[g * 8 : g * 8 + 4] + part[g * 8 + 4 : g * 8 + 8]
                tile = jnp.concatenate([both[0:1] + both[1:2], both[2:3] + both[3:4]], axis=0)
                width = min(LANES, PACK - j * LANES)
                out_ref[g * slots + slot, :, j * LANES : j * LANES + width] = tile[:, :width]


def call(kernel, name, out_shape, operands, scratch=(), scalars=0):
    operands = [
        x if i < scalars else pltpu.with_memory_space_constraint(x, pltpu.VMEM)
        for i, x in enumerate(operands)
    ]
    return pl.pallas_call(
        kernel,
        out_shape=tuple(pltpu.VMEM(shape, dtype) for shape, dtype in out_shape),
        in_specs=[
            pl.BlockSpec(memory_space=pltpu.SMEM if i < scalars else pltpu.VMEM)
            for i in range(len(operands))
        ],
        out_specs=(pl.BlockSpec(memory_space=pltpu.VMEM),) * len(out_shape),
        scratch_shapes=scratch,
        compiler_params=pltpu.CompilerParams(vmem_limit_bytes=SCOPED),
        name=name,
    )(*operands)


def two_parts(matrix):
    upper = jnp.asarray(matrix).astype(BF16)
    return upper, (matrix - upper.astype(F32)).astype(BF16)


def trig_table(pair_slots, owners, slot_dev, matrices):
    pairs = pair_slots.reshape(owners, 1, slot_dev)
    orders = jnp.concatenate([pairs, LMAX - pairs], axis=1).reshape(-1, 1)
    span = lax.broadcasted_iota(jnp.int32, (1, LANES), 1)
    coarse = (orders * (span * LANES)) % NPHI
    fine = (orders * span) % NPHI
    scale = 2.0 * math.pi / NPHI
    coarse = coarse.astype(F32) * scale
    fine = fine.astype(F32) * scale
    shape = (2 * orders.shape[0], NPHI)
    trig = (jnp.cos(coarse), jnp.sin(coarse), jnp.cos(fine), jnp.sin(fine))
    made = [(shape, BF16)] + [(m.shape, BF16) for m in matrices]
    return call(table_kernel, "table", made, trig + matrices)


def local(spectra, legendre, pair_slots, theta_owner):
    slot_dev, _, half = legendre.shape
    owners = lax.axis_size("ma")
    levels = lax.axis_size("row") * spectra.shape[0]
    theta_dev = 2 * half // owners
    groups = half // LANES
    synth_upper, synth_lower = two_parts(chebyshev_pair(levels)[0])
    upper, lower = two_parts(chebyshev_pair(levels)[1])
    matrices = (
        jnp.concatenate([synth_upper, synth_lower], axis=1),
        jnp.concatenate([upper, upper, lower], axis=1),
    )
    made = trig_table(pair_slots, owners, slot_dev, matrices)
    orders = made[0].shape[0]
    theta_row = theta_owner.reshape(1, half)

    vmem = pl.BlockSpec(memory_space=pltpu.VMEM)
    smem = pl.BlockSpec(memory_space=pltpu.SMEM)
    far = pl.BlockSpec(memory_space=pltpu.HBM)
    held = [pltpu.VMEM(legendre.shape, BF16), pltpu.SemaphoreType.DMA((slot_dev,))]
    params = pltpu.CompilerParams(vmem_limit_bytes=LEGENDRE_SCOPED)
    near = lambda x: pltpu.with_memory_space_constraint(x, pltpu.VMEM)

    flat = jnp.transpose(spectra, (0, 1, 2, 4, 3)).reshape(3 * slot_dev, 2, PACK)
    (outgoing,) = pl.pallas_call(
        synthesis_kernel,
        out_shape=(pltpu.VMEM((owners, 6 * slot_dev, LANES), BF16),),
        in_specs=[smem, far, vmem, vmem],
        out_specs=(vmem,),
        scratch_shapes=[pltpu.VMEM((groups, 24 * slot_dev, LANES), F32)] + held,
        compiler_params=params,
        name="synthesis",
    )(pair_slots, legendre, near(flat), near(theta_row))
    rows = lax.all_to_all(outgoing, "ma", split_axis=0, concat_axis=0, tiled=True)
    rows, made = lax.optimization_barrier((rows, made))

    full, rest = divmod(orders, LANES)
    sent = -(-(3 * full + 1) // 2)
    assert 3 * rest <= LANES and 2 * rest <= LANES and theta_dev == levels
    (tiles,) = call(
        turn_kernel,
        "turn",
        [((theta_dev * sent, 2, LANES), BF16)],
        (rows,),
        [pltpu.VMEM((theta_dev * sent * 2, LANES), F32)],
    )
    tiles = lax.all_to_all(tiles, "row", split_axis=0, concat_axis=0, tiled=True)
    taken = -(-(2 * full + 1) // 2)
    back = taken + NPHI // LANES
    (tiles,) = call(
        grid_kernel,
        "grid",
        [((levels * back, 2, LANES), BF16)],
        (tiles,) + tuple(made),
        [
            pltpu.VMEM((levels * sent * 2, LANES), F32),
            pltpu.VMEM((3 * levels, orders), BF16),
            pltpu.VMEM((2 * levels, NPHI), BF16),
            pltpu.VMEM((levels * back * 2, LANES), F32),
        ],
    )
    tiles = lax.all_to_all(tiles, "row", split_axis=0, concat_axis=0, tiled=True)
    (fourier,) = call(
        return_kernel,
        "return",
        [((owners, 4 * slot_dev, 2 * theta_dev), BF16)],
        (tiles,),
        [
            pltpu.VMEM((theta_dev * taken * 2, LANES), F32),
            pltpu.VMEM((orders, 2 * theta_dev), F32),
        ],
    )
    flux = pl.pallas_call(
        flux_kernel,
        out_shape=jax.ShapeDtypeStruct((theta_dev, 2, NPHI), BF16),
        in_specs=[vmem],
        compiler_params=pltpu.CompilerParams(vmem_limit_bytes=SCOPED),
        name="flux",
    )(near(tiles))
    returned = lax.all_to_all(fourier, "ma", split_axis=0, concat_axis=0, tiled=True)
    returned, flux = lax.optimization_barrier((returned, flux))
    result = pl.pallas_call(
        analysis_kernel,
        out_shape=jax.ShapeDtypeStruct((2 * slot_dev, 2, PACK), F32),
        in_specs=[smem, far, vmem, vmem],
        scratch_shapes=[pltpu.VMEM((groups, 16 * slot_dev, LANES), F32)] + held,
        compiler_params=params,
        name="analysis",
    )(pair_slots, legendre, near(returned), near(theta_row))
    result = jnp.transpose(result.reshape(1, 2, slot_dev, 2, PACK), (0, 1, 2, 4, 3))
    return flux[None], result


def solution(mesh):
    in_specs = (P("row", None, "ma", None, None), P("ma", None, None), P(), P())
    out_specs = (P("row", "ma", None, None), P("row", None, "ma", None, None))
    return jax.shard_map(local, mesh=mesh, in_specs=in_specs, out_specs=out_specs, check_vma=False)
```

time: 145 us -> 131 us (0.903); the launches traced: 144 us -> 128 us
  blocking collectives: 84.5 us -> 54.3 us
  waiting for transfers between devices: 13.3 us -> 29.1 us
  Pallas kernels: 14.4 us -> 20.8 us
  local copies, waits for them, and re-layouts: 7.22 us -> 1.87 us
  matrix products: 2.15 us -> 0 us
    all_to_all x4 -> x2, blocking collectives: 84.5 us -> 54.3 us  [local(): lax.all_to_all(tiles, 'row', split_axis=0, concat_axis=0, tiled=True)]
    all_to_all x2, waiting for transfers between devices: 13.3 us -> 29.1 us  [the longest x1 14.7 us: local(): lax.all_to_all(outgoing, 'ma', split_axis=0, concat_axis=0, tiled=True)]
    pallas_call x2, Pallas kernels: 1.58 us -> 6.88 us  [the longest x1 6.1 us: local(): pl.pallas_call(analysis_kernel, out_shape=jax.ShapeDtypeStruct((2 * slot_...]
    reshape x4 -> x0, local copies, waits for them, and re-layouts: 2.53 us -> none  [the longest x2 1.7 us: level_mix(): mixed = mixed.reshape(levels * share, 2, LANES)]
    dot_general x2 -> x0, matrix products: 2.15 us -> none  [level_mix(): mixed = jnp.dot(matrix, here, precision=HIGH).astype(BF16)]
    unnamed x9 -> x8, local copies, waits for them, and re-layouts: 3.13 us -> 0.99 us
    pallas_call x3 -> x4, Pallas kernels: 7.56 us -> 7.76 us  [call(): pl.pallas_call(kernel, out_shape=tuple((pltpu.VMEM(shape, dtype) for shap...]
  transfers between devices with their start and end apart: 2 -> 2, of which waited for: 2 -> 2; matrix products, arithmetic and copies ran while one was open for 4% -> 2% of each run, Pallas kernels for 1% -> 2%
where the time goes in v4:
time: 131 us; the launch traced here: 128 us
  blocking collectives  54.3 us (41%)
  waiting for transfers between devices  29.1 us (22%)
  Pallas kernels  20.8 us (16%)
  starting transfers between devices  19.3 us (15%)
  other arithmetic  2.27 us (2%)
  local copies, waits for them, and re-layouts  1.87 us (1%)
    all_to_all x2, blocking collectives, local(): lax.all_to_all(tiles, 'row', split_axis=0, concat_axis=0, tiled=True)  54.3 us
    all_to_all x1, starting transfers between devices, local(): lax.all_to_all(outgoing, 'ma', split_axis=0, concat_axis=0, tiled=True)  15.7 us
    all_to_all x1, waiting for transfers between devices, local(): lax.all_to_all(outgoing, 'ma', split_axis=0, concat_axis=0, tiled=True)  14.7 us
    all_to_all x1, waiting for transfers between devices, local(): lax.all_to_all(fourier, 'ma', split_axis=0, concat_axis=0, tiled=True)  14.4 us
    pallas_call x4, Pallas kernels, call(): pl.pallas_call(kernel, out_shape=tuple((pltpu.VMEM(shape, dtype) for shap...  7.76 us
    pallas_call x1, Pallas kernels, local(): pl.pallas_call(synthesis_kernel, out_shape=(pltpu.VMEM((owners, 6 * slot_...  6.18 us
    pallas_call x1, Pallas kernels, local(): pl.pallas_call(analysis_kernel, out_shape=jax.ShapeDtypeStruct((2 * slot_...  6.1 us
    all_to_all x1, starting transfers between devices, local(): lax.all_to_all(fourier, 'ma', split_axis=0, concat_axis=0, tiled=True)  3.54 us
  transfers between devices with their start and end apart: 2, of which 2 were waited for; matrix products, arithmetic and copies ran while one was open for 2% of the time, Pallas kernels for 2%

profile of v4, /device:TPU:1, one launch (start us, length us, event | category | flops | bytes accessed | tf_op | source)
XLA Modules:
  0.0 128.4 jit_solution(11029108464374216199)
XLA Ops:
  0.6 0.0 copy-start.3
  0.6 0.7 reshape.36.theta_ref
  1.3 0.0 copy-start
  1.3 1.0 copy-done
  2.3 0.0 copy-start.1
  2.3 0.0 copy-start.2
  2.3 6.2 %synthesis.1 = bf16[12,132,128]{2,1,0:T(8,128)(2,1)} custom-call(s32[264]{0:T(512)} %pairs_ref.3, bf16[22,513,384]{2,1,0:T(8,128)(2,1)} %source_ref.3, f32[66,2,513]{2,1,0:T(2,128)S(1)} %bitcast.7, s32[1,384]{1,0:T(1,128)S(1)} %reshape.36.theta_ref), custom_call_target="tpu_custom_call" | custom-call | tf_op jit(solution)/shard_map/synthesis/pallas_call | solution.py:373
  8.5 15.7 %all-to-all-start = ((bf16[12,132,128]{2,1,0:T(8,128)(2,1)}), bf16[12,132,128]{2,1,0:T(8,128)(2,1)}, u32[]{:S(2)}, u32[]{:S(2)}) async-start(bf16[12,132,128]{2,1,0:T(8,128)(2,1)} %synthesis.1), calls=%async_computation | async-start | bytes 835584 | tf_op jit(solution)/shard_map/all_to_all | solution.py:382
  24.2 0.0 copy-done.3
  24.3 0.1 reshape.37
  24.4 0.1 mul.43
  24.5 2.2 %fusion.10 = (f32[528,128]{1,0:T(8,128)S(1)}, f32[528,128]{1,0:T(8,128)S(1)}, f32[528,128]{1,0:T(8,128)S(1)}, f32[528,128]{1,0:T(8,128)S(1)}) fusion(s32[128]{0:T(128)S(1)} %iota_multiply_fusion, s32[528]{0:T(1024)S(1)} %mul.43), kind=kLoop, calls=%fused_computation.14 | loop fusion | flops 1216512 | bytes 1083968 | tf_op jit(solution)/shard_map/sin | solution.py:344
  26.8 0.0 copy-done.1
  26.8 0.0 copy-done.2
  26.8 2.1 %table.1 = (bf16[1056,1536]{1,0:T(8,128)(2,1)S(1)}, bf16[64,128]{1,0:T(8,128)(2,1)S(1)}, bf16[64,192]{1,0:T(8,128)(2,1)S(1)}) custom-call(f32[528,128]{1,0:T(8,128)S(1)} %get-tuple-element.21.coarse_cos_ref, f32[528,128]{1,0:T(8,128)S(1)} %get-tuple-element.20.coarse_sin_ref, f32[528,128]{1,0:T(8,128)S(1)} %get-tuple-element.23.fine_cos_ref, ...), custom_call_target="tpu_custom_call" | custom-call | tf_op jit(solution)/shard_map/table/pallas_call | solution.py:315
  28.8 14.7 %all-to-all-done.rows_ref = bf16[12,132,128]{2,1,0:T(8,128)(2,1)} async-done(((bf16[12,132,128]{2,1,0:T(8,128)(2,1)}), bf16[12,132,128]{2,1,0:T(8,128)(2,1)}, u32[]{:S(2)}, u32[]{:S(2)}) %all-to-all-start) | async-done | bytes 405536 | tf_op jit(solution)/shard_map/all_to_all | solution.py:382
  43.5 1.6 %turn.1 = bf16[832,2,128]{2,1,0:T(2,128)(2,1)S(1)} custom-call(bf16[12,132,128]{2,1,0:T(8,128)(2,1)} %all-to-all-done.rows_ref), custom_call_target="tpu_custom_call" | custom-call | tf_op jit(solution)/shard_map/turn/pallas_call | solution.py:315
  45.1 27.4 %all_to_all.20.tiles_ref = bf16[832,2,128]{2,1,0:T(2,128)(2,1)S(1)} all-to-all(bf16[832,2,128]{2,1,0:T(2,128)(2,1)S(1)} %turn.1), channel_id=1, replica_groups=mesh['ma'=12,'row'=64] {'row'}, dimensions={0} | all-to-all | bytes 851968 | tf_op jit(solution)/shard_map/all_to_all | solution.py:395
  72.5 3.1 %grid.1 = bf16[1344,2,128]{2,1,0:T(2,128)(2,1)S(1)} custom-call(bf16[832,2,128]{2,1,0:T(2,128)(2,1)S(1)} %all_to_all.20.tiles_ref, bf16[1056,1536]{1,0:T(8,128)(2,1)S(1)} %get-tuple-element.15.table_ref, bf16[64,128]{1,0:T(8,128)(2,1)S(1)} %get-tuple-element.16.synth_ref, bf16[64,192]{1,0:T(8,128)(2,1)S(1)} %get-tuple-element.17.analysis_ref), custom_call_target="tpu_custom_call" | custom-call | tf_op jit(solution)/shard_map/grid/pallas_call | solution.py:315
  75.6 27.0 %all_to_all.21.tiles_ref = bf16[1344,2,128]{2,1,0:T(2,128)(2,1)S(1)} all-to-all(bf16[1344,2,128]{2,1,0:T(2,128)(2,1)S(1)} %grid.1), channel_id=1, replica_groups=mesh['ma'=12,'row'=64] {'row'}, dimensions={0} | all-to-all | bytes 1376256 | tf_op jit(solution)/shard_map/all_to_all | solution.py:410
  102.6 1.1 return.1
  103.6 3.5 %all-to-all-start.3 = ((bf16[12,88,128]{2,1,0:T(8,128)(2,1)}), bf16[12,88,128]{2,1,0:T(8,128)(2,1)S(1)}, u32[]{:S(2)}, u32[]{:S(2)}) async-start(bf16[12,88,128]{2,1,0:T(8,128)(2,1)} %return.1), calls=%async_computation.3 | async-start | bytes 540672 | tf_op jit(solution)/shard_map/all_to_all | solution.py:428
  107.2 0.8 flux.1
  107.9 14.4 %all-to-all-done.3.rows_ref = bf16[12,88,128]{2,1,0:T(8,128)(2,1)S(1)} async-done(((bf16[12,88,128]{2,1,0:T(8,128)(2,1)}), bf16[12,88,128]{2,1,0:T(8,128)(2,1)S(1)}, u32[]{:S(2)}, u32[]{:S(2)}) %all-to-all-start.3) | async-done | bytes 270368 | tf_op jit(solution)/shard_map/all_to_all | solution.py:428
  122.3 6.1 %analysis.1 = f32[44,2,513]{2,1,0:T(2,128)} custom-call(s32[264]{0:T(512)} %pairs_ref.3, bf16[22,513,384]{2,1,0:T(8,128)(2,1)} %source_ref.3, bf16[12,88,128]{2,1,0:T(8,128)(2,1)S(1)} %all-to-all-done.3.rows_ref, s32[1,384]{1,0:T(1,128)S(1)} %reshape.36.theta_ref), custom_call_target="tpu_custom_call" | custom-call | tf_op jit(solution)/shard_map/analysis/pallas_call | solution.py:430
  (3 shorter events, 0.0 us)
Async XLA Ops:
  0.6 23.6 %copy-start.3 = (s32[264]{0:T(512)S(1)}, s32[264]{0:T(512)}, u32[]{:S(2)}) copy-start(s32[264]{0:T(512)} %pairs_ref.3) | copy-start | bytes 3172
  1.3 1.0 copy-start
  2.3 24.4 %copy-start.1 = (bf16[64,192]{1,0:T(8,128)(2,1)S(1)}, bf16[64,192]{1,0:T(8,128)(2,1)}, u32[]{:S(2)}) copy-start(bf16[64,192]{1,0:T(8,128)(2,1)} %constant.38.analysis_ref) | copy-start | bytes 73732
  2.3 24.5 %copy-start.2 = (bf16[64,128]{1,0:T(8,128)(2,1)S(1)}, bf16[64,128]{1,0:T(8,128)(2,1)}, u32[]{:S(2)}) copy-start(bf16[64,128]{1,0:T(8,128)(2,1)} %constant.33.synth_ref) | copy-start | bytes 49156
  8.5 35.0 %all-to-all-start = ((bf16[12,132,128]{2,1,0:T(8,128)(2,1)}), bf16[12,132,128]{2,1,0:T(8,128)(2,1)}, u32[]{:S(2)}, u32[]{:S(2)}) async-start(bf16[12,132,128]{2,1,0:T(8,128)(2,1)} %synthesis.1), calls=%async_computation | async-start | bytes 835584 | tf_op jit(solution)/shard_map/all_to_all | solution.py:382
  103.6 18.7 %all-to-all-start.3 = ((bf16[12,88,128]{2,1,0:T(8,128)(2,1)}), bf16[12,88,128]{2,1,0:T(8,128)(2,1)S(1)}, u32[]{:S(2)}, u32[]{:S(2)}) async-start(bf16[12,88,128]{2,1,0:T(8,128)(2,1)} %return.1), calls=%async_computation.3 | async-start | bytes 540672 | tf_op jit(solution)/shard_map/all_to_all | solution.py:428

commit v5 on v4

--- a/solution.py
+++ b/solution.py
@@ -18,7 +18,9 @@
 WIDTH = 256
 SCOPED = 16 << 20
 LEGENDRE_SCOPED = 56 << 20
+SYNTHESIS_SCOPED = 65300 << 10
 GROUP = 4
+AHEAD = 8
 BF16 = jnp.bfloat16
 F32 = jnp.float32
 NT = (((1,), (1,)), ((), ()))
@@ -32,10 +34,10 @@
     return cosines.astype(np.float32), analysis.astype(np.float32)
 
 
-def one_hot(theta_row):
-    half = theta_row.shape[1]
+def one_hot(theta):
+    half = theta.shape[0]
     natural = lax.broadcasted_iota(jnp.int32, (half, half), 0)
-    return jnp.where(natural == theta_row, 1.0, 0.0).astype(BF16)
+    return jnp.where(natural == theta.reshape(1, half), 1.0, 0.0).astype(BF16)
 
 
 def slot_masks(pair, column, order_odd):
@@ -47,30 +49,38 @@
     return jnp.where(order_odd, high, low), jnp.where(order_odd, high_sign, low_sign)
 
 
-def start_copies(source_ref, table_ref, arrived):
+def slot_copies(source_ref, table_ref, arrived):
     copies = [
         pltpu.make_async_copy(source_ref.at[slot], table_ref.at[slot], arrived.at[slot])
         for slot in range(table_ref.shape[0])
     ]
-    for copy in copies:
+    for copy in copies[:AHEAD]:
         copy.start()
     return copies
 
 
 def wait_group(copies, slot):
     if slot == 0 or (slot - 2) % GROUP == 0:
-        for copy in copies[slot : slot + GROUP if slot else 2]:
+        end = slot + GROUP if slot else 2
+        for copy in copies[slot:end]:
             copy.wait()
+        for copy in copies[slot + AHEAD : end + AHEAD]:
+            copy.start()
 
 
 def synthesis_kernel(
-    pairs_ref, source_ref, spectra_ref, theta_ref, out_ref, rows_ref, table_ref, arrived
+    pairs_ref, source_ref, given_ref, owner_ref, out_ref,
+    rows_ref, spectra_ref, theta_ref, here, table_ref, arrived,
 ):
     slots = table_ref.shape[0]
-    copies = start_copies(source_ref, table_ref, arrived)
+    given = pltpu.make_async_copy(given_ref, spectra_ref, here.at[0])
+    owner = pltpu.make_async_copy(owner_ref, theta_ref, here.at[1])
+    given.start()
+    owner.start()
+    copies = slot_copies(source_ref, table_ref, arrived)
     first = lax.axis_index("ma") * slots
     owners = out_ref.shape[0]
-    own_half = theta_ref.shape[1] // owners
+    own_half = theta_ref.shape[0] // owners
     groups = rows_ref.shape[0]
     block = 6 * slots
     row = lax.broadcasted_iota(jnp.int32, (8, LANES), 0)
@@ -79,6 +89,9 @@
     lane = lax.broadcasted_iota(jnp.int32, (8, LANES), 1)
 
     for slot in range(slots):
+        if slot == 0:
+            given.wait()
+            owner.wait()
         wait_group(copies, slot)
         pair = pairs_ref[first + slot]
         weight = jnp.where((pair == 0) & (row & 1 == 0), 1.0, 2.0)
@@ -265,10 +278,10 @@
     pairs_ref, source_ref, rows_ref, theta_ref, out_ref, nat_ref, table_ref, arrived
 ):
     slots = table_ref.shape[0]
-    copies = start_copies(source_ref, table_ref, arrived)
+    copies = slot_copies(source_ref, table_ref, arrived)
     first = lax.axis_index("ma") * slots
     owners = rows_ref.shape[0]
-    own_half = theta_ref.shape[1] // owners
+    own_half = theta_ref.shape[0] // owners
     block = rows_ref.shape[1]
     groups = nat_ref.shape[0]
     select = one_hot(theta_ref[...])
@@ -360,7 +373,6 @@
     )
     made = trig_table(pair_slots, owners, slot_dev, matrices)
     orders = made[0].shape[0]
-    theta_row = theta_owner.reshape(1, half)
 
     vmem = pl.BlockSpec(memory_space=pltpu.VMEM)
     smem = pl.BlockSpec(memory_space=pltpu.SMEM)
@@ -370,15 +382,20 @@
     near = lambda x: pltpu.with_memory_space_constraint(x, pltpu.VMEM)
 
     flat = jnp.transpose(spectra, (0, 1, 2, 4, 3)).reshape(3 * slot_dev, 2, PACK)
-    (outgoing,) = pl.pallas_call(
+    outgoing = pl.pallas_call(
         synthesis_kernel,
-        out_shape=(pltpu.VMEM((owners, 6 * slot_dev, LANES), BF16),),
-        in_specs=[smem, far, vmem, vmem],
-        out_specs=(vmem,),
-        scratch_shapes=[pltpu.VMEM((groups, 24 * slot_dev, LANES), F32)] + held,
-        compiler_params=params,
+        out_shape=jax.ShapeDtypeStruct((owners, 6 * slot_dev, LANES), BF16),
+        in_specs=[smem, far, far, far],
+        scratch_shapes=[
+            pltpu.VMEM((groups, 24 * slot_dev, LANES), F32),
+            pltpu.VMEM(flat.shape, F32),
+            pltpu.VMEM(theta_owner.shape, jnp.int32),
+            pltpu.SemaphoreType.DMA((2,)),
+        ]
+        + held,
+        compiler_params=pltpu.CompilerParams(vmem_limit_bytes=SYNTHESIS_SCOPED),
         name="synthesis",
-    )(pair_slots, legendre, near(flat), near(theta_row))
+    )(pair_slots, legendre, flat, theta_owner)
     rows = lax.all_to_all(outgoing, "ma", split_axis=0, concat_axis=0, tiled=True)
     rows, made = lax.optimization_barrier((rows, made))
 
@@ -434,7 +451,7 @@
         scratch_shapes=[pltpu.VMEM((groups, 16 * slot_dev, LANES), F32)] + held,
         compiler_params=params,
         name="analysis",
-    )(pair_slots, legendre, near(returned), near(theta_row))
+    )(pair_slots, legendre, near(returned), near(theta_owner))
     result = jnp.transpose(result.reshape(1, 2, slot_dev, 2, PACK), (0, 1, 2, 4, 3))
     return flux[None], result
 

time: 131 us -> 132 us (level)
  Pallas kernels: 20.8 us -> 23.2 us
  local copies, waits for them, and re-layouts: 1.87 us -> 0.21 us
    pallas_call x1, Pallas kernels: 6.18 us -> 7.54 us  [local(): pl.pallas_call(synthesis_kernel, out_shape=jax.ShapeDtypeStruct((owners,...]
where the time goes in v5:
time: 132 us; the launch traced here: 129 us
  blocking collectives  54.3 us (41%)
  waiting for transfers between devices  29 us (22%)
  Pallas kernels  23.2 us (18%)
  starting transfers between devices  19.5 us (15%)
  other arithmetic  2.27 us (2%)
    all_to_all x2, blocking collectives, local(): lax.all_to_all(tiles, 'row', split_axis=0, concat_axis=0, tiled=True)  54.3 us
    all_to_all x1, starting transfers between devices, local(): lax.all_to_all(outgoing, 'ma', split_axis=0, concat_axis=0, tiled=True)  15.7 us
    all_to_all x1, waiting for transfers between devices, local(): lax.all_to_all(outgoing, 'ma', split_axis=0, concat_axis=0, tiled=True)  14.6 us
    all_to_all x1, waiting for transfers between devices, local(): lax.all_to_all(fourier, 'ma', split_axis=0, concat_axis=0, tiled=True)  14.4 us
    pallas_call x4, Pallas kernels, call(): pl.pallas_call(kernel, out_shape=tuple((pltpu.VMEM(shape, dtype) for shap...  7.94 us
    pallas_call x1, Pallas kernels, local(): pl.pallas_call(synthesis_kernel, out_shape=jax.ShapeDtypeStruct((owners,...  7.54 us
    pallas_call x1, Pallas kernels, local(): pl.pallas_call(analysis_kernel, out_shape=jax.ShapeDtypeStruct((2 * slot_...  6.91 us
    all_to_all x1, starting transfers between devices, local(): lax.all_to_all(fourier, 'ma', split_axis=0, concat_axis=0, tiled=True)  3.72 us
  transfers between devices with their start and end apart: 2, of which 2 were waited for; matrix products, arithmetic and copies ran while one was open for 2% of the time, Pallas kernels for 2%

profile of v5, /device:TPU:1, one launch (start us, length us, event | category | flops | bytes accessed | tf_op | source)
XLA Modules:
  0.0 129.3 jit_solution(6393232140812924162)
XLA Ops:
  0.6 0.0 copy-start.1
  0.6 0.0 copy-start
  0.7 0.0 copy-start.3
  0.7 7.5 %synthesis.1 = bf16[12,132,128]{2,1,0:T(8,128)(2,1)} custom-call(s32[264]{0:T(512)} %pairs_ref.3, bf16[22,513,384]{2,1,0:T(8,128)(2,1)} %source_ref.3, f32[66,2,513]{2,1,0:T(2,128)} %bitcast.8, s32[384]{0:T(512)} %theta_ref.1), custom_call_target="tpu_custom_call" | custom-call | tf_op jit(solution)/shard_map/synthesis/pallas_call | solution.py:385
  8.2 0.0 copy-start.2
  8.2 15.7 %all-to-all-start = ((bf16[12,132,128]{2,1,0:T(8,128)(2,1)}), bf16[12,132,128]{2,1,0:T(8,128)(2,1)}, u32[]{:S(2)}, u32[]{:S(2)}) async-start(bf16[12,132,128]{2,1,0:T(8,128)(2,1)} %synthesis.1), calls=%async_computation | async-start | bytes 835584 | tf_op jit(solution)/shard_map/all_to_all | solution.py:399
  24.0 0.0 copy-done.3
  24.0 0.1 reshape.33
  24.1 0.1 mul.43
  24.2 2.2 %fusion.10 = (f32[528,128]{1,0:T(8,128)S(1)}, f32[528,128]{1,0:T(8,128)S(1)}, f32[528,128]{1,0:T(8,128)S(1)}, f32[528,128]{1,0:T(8,128)S(1)}) fusion(s32[128]{0:T(128)S(1)} %iota_multiply_fusion, s32[528]{0:T(1024)S(1)} %mul.43), kind=kLoop, calls=%fused_computation.14 | loop fusion | flops 1216512 | bytes 1083968 | tf_op jit(solution)/shard_map/sin | solution.py:357
  26.5 0.0 copy-done.1
  26.5 0.0 copy-done
  26.5 2.2 %table.1 = (bf16[1056,1536]{1,0:T(8,128)(2,1)S(1)}, bf16[64,128]{1,0:T(8,128)(2,1)S(1)}, bf16[64,192]{1,0:T(8,128)(2,1)S(1)}) custom-call(f32[528,128]{1,0:T(8,128)S(1)} %get-tuple-element.21.coarse_cos_ref, f32[528,128]{1,0:T(8,128)S(1)} %get-tuple-element.20.coarse_sin_ref, f32[528,128]{1,0:T(8,128)S(1)} %get-tuple-element.23.fine_cos_ref, ...), custom_call_target="tpu_custom_call" | custom-call | tf_op jit(solution)/shard_map/table/pallas_call | solution.py:328
  28.7 14.6 %all-to-all-done.rows_ref = bf16[12,132,128]{2,1,0:T(8,128)(2,1)} async-done(((bf16[12,132,128]{2,1,0:T(8,128)(2,1)}), bf16[12,132,128]{2,1,0:T(8,128)(2,1)}, u32[]{:S(2)}, u32[]{:S(2)}) %all-to-all-start) | async-done | bytes 405536 | tf_op jit(solution)/shard_map/all_to_all | solution.py:399
  43.3 1.6 %turn.1 = bf16[832,2,128]{2,1,0:T(2,128)(2,1)S(1)} custom-call(bf16[12,132,128]{2,1,0:T(8,128)(2,1)} %all-to-all-done.rows_ref), custom_call_target="tpu_custom_call" | custom-call | tf_op jit(solution)/shard_map/turn/pallas_call | solution.py:328
  44.9 27.4 %all_to_all.20.tiles_ref = bf16[832,2,128]{2,1,0:T(2,128)(2,1)S(1)} all-to-all(bf16[832,2,128]{2,1,0:T(2,128)(2,1)S(1)} %turn.1), channel_id=1, replica_groups=mesh['ma'=12,'row'=64] {'row'}, dimensions={0} | all-to-all | bytes 851968 | tf_op jit(solution)/shard_map/all_to_all | solution.py:412
  72.2 3.1 %grid.1 = bf16[1344,2,128]{2,1,0:T(2,128)(2,1)S(1)} custom-call(bf16[832,2,128]{2,1,0:T(2,128)(2,1)S(1)} %all_to_all.20.tiles_ref, bf16[1056,1536]{1,0:T(8,128)(2,1)S(1)} %get-tuple-element.15.table_ref, bf16[64,128]{1,0:T(8,128)(2,1)S(1)} %get-tuple-element.16.synth_ref, bf16[64,192]{1,0:T(8,128)(2,1)S(1)} %get-tuple-element.17.analysis_ref), custom_call_target="tpu_custom_call" | custom-call | tf_op jit(solution)/shard_map/grid/pallas_call | solution.py:328
  75.4 26.9 %all_to_all.21.tiles_ref = bf16[1344,2,128]{2,1,0:T(2,128)(2,1)S(1)} all-to-all(bf16[1344,2,128]{2,1,0:T(2,128)(2,1)S(1)} %grid.1), channel_id=1, replica_groups=mesh['ma'=12,'row'=64] {'row'}, dimensions={0} | all-to-all | bytes 1376256 | tf_op jit(solution)/shard_map/all_to_all | solution.py:427
  102.3 1.1 return.1
  103.4 3.7 %all-to-all-start.3 = ((bf16[12,88,128]{2,1,0:T(8,128)(2,1)}), bf16[12,88,128]{2,1,0:T(8,128)(2,1)S(1)}, u32[]{:S(2)}, u32[]{:S(2)}) async-start(bf16[12,88,128]{2,1,0:T(8,128)(2,1)} %return.1), calls=%async_computation.3 | async-start | bytes 540672 | tf_op jit(solution)/shard_map/all_to_all | solution.py:445
  107.1 0.8 flux.1
  107.9 14.4 %all-to-all-done.3.rows_ref = bf16[12,88,128]{2,1,0:T(8,128)(2,1)S(1)} async-done(((bf16[12,88,128]{2,1,0:T(8,128)(2,1)}), bf16[12,88,128]{2,1,0:T(8,128)(2,1)S(1)}, u32[]{:S(2)}, u32[]{:S(2)}) %all-to-all-start.3) | async-done | bytes 270368 | tf_op jit(solution)/shard_map/all_to_all | solution.py:445
  122.3 0.0 copy-done.2
  122.3 6.9 %analysis.1 = f32[44,2,513]{2,1,0:T(2,128)} custom-call(s32[264]{0:T(512)} %pairs_ref.3, bf16[22,513,384]{2,1,0:T(8,128)(2,1)} %source_ref.3, bf16[12,88,128]{2,1,0:T(8,128)(2,1)S(1)} %all-to-all-done.3.rows_ref, s32[384]{0:T(512)S(1)} %copy-done.2), custom_call_target="tpu_custom_call" | custom-call | tf_op jit(solution)/shard_map/analysis/pallas_call | solution.py:447
  (3 shorter events, 0.0 us)
Async XLA Ops:
  0.6 25.9 %copy-start.1 = (bf16[64,128]{1,0:T(8,128)(2,1)S(1)}, bf16[64,128]{1,0:T(8,128)(2,1)}, u32[]{:S(2)}) copy-start(bf16[64,128]{1,0:T(8,128)(2,1)} %constant.33.synth_ref) | copy-start | bytes 49156
  0.6 25.8 %copy-start = (bf16[64,192]{1,0:T(8,128)(2,1)S(1)}, bf16[64,192]{1,0:T(8,128)(2,1)}, u32[]{:S(2)}) copy-start(bf16[64,192]{1,0:T(8,128)(2,1)} %constant.38.analysis_ref) | copy-start | bytes 73732
  0.7 23.3 %copy-start.3 = (s32[264]{0:T(512)S(1)}, s32[264]{0:T(512)}, u32[]{:S(2)}) copy-start(s32[264]{0:T(512)} %pairs_ref.3) | copy-start | bytes 3172
  8.2 114.1 %copy-start.2 = (s32[384]{0:T(512)S(1)}, s32[384]{0:T(512)}, u32[]{:S(2)}) copy-start(s32[384]{0:T(512)} %theta_ref.1) | copy-start | bytes 4612
  8.2 35.1 %all-to-all-start = ((bf16[12,132,128]{2,1,0:T(8,128)(2,1)}), bf16[12,132,128]{2,1,0:T(8,128)(2,1)}, u32[]{:S(2)}, u32[]{:S(2)}) async-start(bf16[12,132,128]{2,1,0:T(8,128)(2,1)} %synthesis.1), calls=%async_computation | async-start | bytes 835584 | tf_op jit(solution)/shard_map/all_to_all | solution.py:399
  103.4 18.9 %all-to-all-start.3 = ((bf16[12,88,128]{2,1,0:T(8,128)(2,1)}), bf16[12,88,128]{2,1,0:T(8,128)(2,1)S(1)}, u32[]{:S(2)}, u32[]{:S(2)}) async-start(bf16[12,88,128]{2,1,0:T(8,128)(2,1)} %return.1), calls=%async_computation.3 | async-start | bytes 540672 | tf_op jit(solution)/shard_map/all_to_all | solution.py:445

commit v6 on v5

--- a/solution.py
+++ b/solution.py
@@ -20,7 +20,7 @@
 LEGENDRE_SCOPED = 56 << 20
 SYNTHESIS_SCOPED = 65300 << 10
 GROUP = 4
-AHEAD = 8
+FIRST = 6
 BF16 = jnp.bfloat16
 F32 = jnp.float32
 NT = (((1,), (1,)), ((), ()))
@@ -54,23 +54,18 @@
         pltpu.make_async_copy(source_ref.at[slot], table_ref.at[slot], arrived.at[slot])
         for slot in range(table_ref.shape[0])
     ]
-    for copy in copies[:AHEAD]:
+    for copy in copies[:FIRST]:
         copy.start()
     return copies
 
 
-def wait_group(copies, slot):
-    if slot == 0 or (slot - 2) % GROUP == 0:
-        end = slot + GROUP if slot else 2
-        for copy in copies[slot:end]:
-            copy.wait()
-        for copy in copies[slot + AHEAD : end + AHEAD]:
-            copy.start()
+def slot_groups(slots):
+    return [(0, 2)] + [(s, min(s + GROUP, slots)) for s in range(2, slots, GROUP)]
 
 
 def synthesis_kernel(
-    pairs_ref, source_ref, given_ref, owner_ref, out_ref,
-    rows_ref, spectra_ref, theta_ref, here, table_ref, arrived,
+    pairs_ref, source_ref, given_ref, owner_ref, result_ref,
+    rows_ref, spectra_ref, theta_ref, here, out_ref, gone, table_ref, arrived,
 ):
     slots = table_ref.shape[0]
     given = pltpu.make_async_copy(given_ref, spectra_ref, here.at[0])
@@ -88,16 +83,12 @@
     field = row >> 1
     lane = lax.broadcasted_iota(jnp.int32, (8, LANES), 1)
 
-    for slot in range(slots):
-        if slot == 0:
-            given.wait()
-            owner.wait()
-        wait_group(copies, slot)
+    def left_of(slot):
         pair = pairs_ref[first + slot]
         weight = jnp.where((pair == 0) & (row & 1 == 0), 1.0, 2.0)
         blocks = [[], [], [], []]
+        picked = [f * slots + slot for f in range(3)]
         for j in range(TILES):
-            picked = [f * slots + slot for f in range(3)]
             if j < TILES - 1:
                 tiles = [spectra_ref[i, :, j * LANES : (j + 1) * LANES] for i in picked]
             else:
@@ -113,26 +104,53 @@
                 blocks[2 * c].append(base)
                 blocks[2 * c + 1].append(base * sign)
         left = jnp.concatenate([jnp.concatenate(b, axis=1) for b in blocks], axis=0)
-        sums = jnp.dot(
-            left[:, :FULL].astype(BF16), table_ref[slot, :FULL, :], preferred_element_type=F32
-        )
-        sums = sums + left[:, FULL : FULL + 1] * table_ref[slot, FULL:PACK, :].astype(F32)
+        return left[:, :FULL].astype(BF16), left[:, FULL : FULL + 1]
+
+    def sums_of(slot, left):
+        sums = jnp.dot(left[0], table_ref[slot, :FULL, :], preferred_element_type=F32)
+        return sums + left[1] * table_ref[slot, FULL:PACK, :].astype(F32)
+
+    def keep(slot, sums):
         for k in range(4):
             for g in range(groups):
                 rows_ref[g, pl.ds(k * block + slot, 6, stride=slots), :] = sums[
                     k * 8 : k * 8 + 6, g * LANES : (g + 1) * LANES
                 ]
+
+    given.wait()
+    owner.wait()
+    for copy in copies[FIRST:]:
+        copy.start()
+    batches = slot_groups(slots)
+    lefts = [left_of(slot) for slot in range(*batches[0])]
     select = one_hot(theta_ref[...])
+    done = []
+    for number, (start, end) in enumerate(batches):
+        for copy in copies[start:end]:
+            copy.wait()
+        made = [(slot, sums_of(slot, lefts[slot - start])) for slot in range(start, end)]
+        if number + 1 < len(batches):
+            lefts = [left_of(slot) for slot in range(*batches[number + 1])]
+        for slot, sums in done:
+            keep(slot, sums)
+        done = made
+    for slot, sums in done:
+        keep(slot, sums)
     moved = []
     for k in range(4):
         rows = jnp.concatenate(
             [rows_ref[g, k * block : (k + 1) * block, :] for g in range(groups)], axis=1
         ).astype(BF16)
         moved.append(jnp.dot(rows, select, preferred_element_type=F32))
+    sent = []
     for d in range(owners):
         out_ref[d] = jnp.concatenate(
             [m[:, d * own_half : (d + 1) * own_half] for m in moved], axis=1
         ).astype(BF16)
+        sent.append(pltpu.make_async_copy(out_ref.at[d], result_ref.at[d], gone.at[d]))
+        sent[-1].start()
+    for copy in sent:
+        copy.wait()
 
 
 def table_kernel(
@@ -275,7 +293,8 @@
 
 
 def analysis_kernel(
-    pairs_ref, source_ref, rows_ref, theta_ref, out_ref, nat_ref, table_ref, arrived
+    pairs_ref, source_ref, rows_ref, theta_ref, result_ref,
+    nat_ref, out_ref, gone, table_ref, arrived,
 ):
     slots = table_ref.shape[0]
     copies = slot_copies(source_ref, table_ref, arrived)
@@ -291,20 +310,25 @@
         nat = lax.dot_general(own.astype(BF16), select, NT, preferred_element_type=F32)
         for g in range(groups):
             nat_ref[g, k * block : (k + 1) * block, :] = nat[:, g * LANES : (g + 1) * LANES]
+    for copy in copies[FIRST:]:
+        copy.start()
+    sent = []
     row = lax.broadcasted_iota(jnp.int32, (16, LANES), 0)
     odd = (row & 1) == 1
     south = (row & 4) == 4
     lane = lax.broadcasted_iota(jnp.int32, (16, LANES), 1)
 
-    for slot in range(slots):
+    def products(slot):
         left = jnp.concatenate(
             [nat_ref[g, pl.ds(slot, 16, stride=slots), :] for g in range(groups)], axis=1
         )
-        wait_group(copies, slot)
         sums = lax.dot_general(
             left.astype(BF16), table_ref[slot, :FULL, :], NT, preferred_element_type=F32
         )
         last = jnp.sum(left * table_ref[slot, FULL:PACK, :].astype(F32), axis=1, keepdims=True)
+        return sums, last
+
+    def finish(slot, sums, last):
         pair = pairs_ref[first + slot]
         for j in range(TILES):
             mask, sign = slot_masks(pair, lane + j * LANES, odd)
@@ -313,11 +337,37 @@
             else:
                 part = jnp.where(lane == 0, last, 0.0)
             part = part * mask * jnp.where(south, sign, 1.0)
+            width = min(LANES, PACK - j * LANES)
             for g in range(2):
                 both = part[g * 8 : g * 8 + 4] + part[g * 8 + 4 : g * 8 + 8]
                 tile = jnp.concatenate([both[0:1] + both[1:2], both[2:3] + both[3:4]], axis=0)
-                width = min(LANES, PACK - j * LANES)
                 out_ref[g * slots + slot, :, j * LANES : j * LANES + width] = tile[:, :width]
+
+    def send(number, start, end):
+        for g in range(2):
+            part = pl.ds(g * slots + start, end - start)
+            copy = pltpu.make_async_copy(
+                out_ref.at[part], result_ref.at[part], gone.at[2 * number + g]
+            )
+            copy.start()
+            sent.append(copy)
+
+    batches = slot_groups(slots)
+    done = []
+    for number, (start, end) in enumerate(batches):
+        for copy in copies[start:end]:
+            copy.wait()
+        made = [(slot, *products(slot)) for slot in range(start, end)]
+        for values in done:
+            finish(*values)
+        if number:
+            send(number - 1, *batches[number - 1])
+        done = made
+    for values in done:
+        finish(*values)
+    send(len(batches) - 1, *batches[-1])
+    for copy in sent:
+        copy.wait()
 
 
 def call(kernel, name, out_shape, operands, scratch=(), scalars=0):
@@ -386,11 +436,14 @@
         synthesis_kernel,
         out_shape=jax.ShapeDtypeStruct((owners, 6 * slot_dev, LANES), BF16),
         in_specs=[smem, far, far, far],
+        out_specs=far,
         scratch_shapes=[
             pltpu.VMEM((groups, 24 * slot_dev, LANES), F32),
             pltpu.VMEM(flat.shape, F32),
             pltpu.VMEM(theta_owner.shape, jnp.int32),
             pltpu.SemaphoreType.DMA((2,)),
+            pltpu.VMEM((owners, 6 * slot_dev, LANES), BF16),
+            pltpu.SemaphoreType.DMA((owners,)),
         ]
         + held,
         compiler_params=pltpu.CompilerParams(vmem_limit_bytes=SYNTHESIS_SCOPED),
@@ -448,7 +501,13 @@
         analysis_kernel,
         out_shape=jax.ShapeDtypeStruct((2 * slot_dev, 2, PACK), F32),
         in_specs=[smem, far, vmem, vmem],
-        scratch_shapes=[pltpu.VMEM((groups, 16 * slot_dev, LANES), F32)] + held,
+        out_specs=far,
+        scratch_shapes=[
+            pltpu.VMEM((groups, 16 * slot_dev, LANES), F32),
+            pltpu.VMEM((2 * slot_dev, 2, PACK), F32),
+            pltpu.SemaphoreType.DMA((2 * len(slot_groups(slot_dev)),)),
+        ]
+        + held,
         compiler_params=params,
         name="analysis",
     )(pair_slots, legendre, near(returned), near(theta_owner))

time: 132 us -> 130 us (0.985)
  no operation moved by 1% of the time
where the time goes in v6:
time: 130 us; the launch traced here: 128 us
  blocking collectives  54.4 us (42%)
  waiting for transfers between devices  28.9 us (22%)
  Pallas kernels  22 us (17%)
  starting transfers between devices  19.3 us (15%)
  other arithmetic  2.27 us (2%)
    all_to_all x2, blocking collectives, local(): lax.all_to_all(tiles, 'row', split_axis=0, concat_axis=0, tiled=True)  54.4 us
    all_to_all x1, starting transfers between devices, local(): lax.all_to_all(outgoing, 'ma', split_axis=0, concat_axis=0, tiled=True)  15.7 us
    all_to_all x1, waiting for transfers between devices, local(): lax.all_to_all(outgoing, 'ma', split_axis=0, concat_axis=0, tiled=True)  14.6 us
    all_to_all x1, waiting for transfers between devices, local(): lax.all_to_all(fourier, 'ma', split_axis=0, concat_axis=0, tiled=True)  14.3 us
    pallas_call x4, Pallas kernels, call(): pl.pallas_call(kernel, out_shape=tuple((pltpu.VMEM(shape, dtype) for shap...  7.93 us
    pallas_call x1, Pallas kernels, local(): pl.pallas_call(synthesis_kernel, out_shape=jax.ShapeDtypeStruct((owners,...  7.12 us
    pallas_call x1, Pallas kernels, local(): pl.pallas_call(analysis_kernel, out_shape=jax.ShapeDtypeStruct((2 * slot_...  6.14 us
    all_to_all x1, starting transfers between devices, local(): lax.all_to_all(fourier, 'ma', split_axis=0, concat_axis=0, tiled=True)  3.54 us
  transfers between devices with their start and end apart: 2, of which 2 were waited for; matrix products, arithmetic and copies ran while one was open for 2% of the time, Pallas kernels for 2%

profile of v6, /device:TPU:1, one launch (start us, length us, event | category | flops | bytes accessed | tf_op | source)
XLA Modules:
  0.0 127.9 jit_solution(8438725069837973941)
XLA Ops:
  0.6 0.0 copy-start.1
  0.6 0.0 copy-start
  0.7 0.0 copy-start.3
  0.7 7.1 %synthesis.1 = bf16[12,132,128]{2,1,0:T(8,128)(2,1)} custom-call(s32[264]{0:T(512)} %pairs_ref.3, bf16[22,513,384]{2,1,0:T(8,128)(2,1)} %source_ref.3, f32[66,2,513]{2,1,0:T(2,128)} %bitcast.8, s32[384]{0:T(512)} %theta_ref.1), custom_call_target="tpu_custom_call" | custom-call | tf_op jit(solution)/shard_map/synthesis/pallas_call | solution.py:435
  7.8 0.0 copy-start.2
  7.8 15.7 %all-to-all-start = ((bf16[12,132,128]{2,1,0:T(8,128)(2,1)}), bf16[12,132,128]{2,1,0:T(8,128)(2,1)}, u32[]{:S(2)}, u32[]{:S(2)}) async-start(bf16[12,132,128]{2,1,0:T(8,128)(2,1)} %synthesis.1), calls=%async_computation | async-start | bytes 835584 | tf_op jit(solution)/shard_map/all_to_all | solution.py:452
  23.5 0.0 copy-done.3
  23.6 0.1 reshape.33
  23.7 0.1 mul.43
  23.8 2.2 %fusion.10 = (f32[528,128]{1,0:T(8,128)S(1)}, f32[528,128]{1,0:T(8,128)S(1)}, f32[528,128]{1,0:T(8,128)S(1)}, f32[528,128]{1,0:T(8,128)S(1)}) fusion(s32[128]{0:T(128)S(1)} %iota_multiply_fusion, s32[528]{0:T(1024)S(1)} %mul.43), kind=kLoop, calls=%fused_computation.14 | loop fusion | flops 1216512 | bytes 1083968 | tf_op jit(solution)/shard_map/sin | solution.py:407
  26.1 0.0 copy-done.1
  26.1 0.0 copy-done
  26.1 2.2 %table.1 = (bf16[1056,1536]{1,0:T(8,128)(2,1)S(1)}, bf16[64,128]{1,0:T(8,128)(2,1)S(1)}, bf16[64,192]{1,0:T(8,128)(2,1)S(1)}) custom-call(f32[528,128]{1,0:T(8,128)S(1)} %get-tuple-element.21.coarse_cos_ref, f32[528,128]{1,0:T(8,128)S(1)} %get-tuple-element.20.coarse_sin_ref, f32[528,128]{1,0:T(8,128)S(1)} %get-tuple-element.23.fine_cos_ref, ...), custom_call_target="tpu_custom_call" | custom-call | tf_op jit(solution)/shard_map/table/pallas_call | solution.py:378
  28.2 14.6 %all-to-all-done.rows_ref = bf16[12,132,128]{2,1,0:T(8,128)(2,1)} async-done(((bf16[12,132,128]{2,1,0:T(8,128)(2,1)}), bf16[12,132,128]{2,1,0:T(8,128)(2,1)}, u32[]{:S(2)}, u32[]{:S(2)}) %all-to-all-start) | async-done | bytes 405536 | tf_op jit(solution)/shard_map/all_to_all | solution.py:452
  42.8 1.6 %turn.1 = bf16[832,2,128]{2,1,0:T(2,128)(2,1)S(1)} custom-call(bf16[12,132,128]{2,1,0:T(8,128)(2,1)} %all-to-all-done.rows_ref), custom_call_target="tpu_custom_call" | custom-call | tf_op jit(solution)/shard_map/turn/pallas_call | solution.py:378
  44.4 27.4 %all_to_all.20.tiles_ref = bf16[832,2,128]{2,1,0:T(2,128)(2,1)S(1)} all-to-all(bf16[832,2,128]{2,1,0:T(2,128)(2,1)S(1)} %turn.1), channel_id=1, replica_groups=mesh['ma'=12,'row'=64] {'row'}, dimensions={0} | all-to-all | bytes 851968 | tf_op jit(solution)/shard_map/all_to_all | solution.py:465
  71.8 3.1 %grid.1 = bf16[1344,2,128]{2,1,0:T(2,128)(2,1)S(1)} custom-call(bf16[832,2,128]{2,1,0:T(2,128)(2,1)S(1)} %all_to_all.20.tiles_ref, bf16[1056,1536]{1,0:T(8,128)(2,1)S(1)} %get-tuple-element.15.table_ref, bf16[64,128]{1,0:T(8,128)(2,1)S(1)} %get-tuple-element.16.synth_ref, bf16[64,192]{1,0:T(8,128)(2,1)S(1)} %get-tuple-element.17.analysis_ref), custom_call_target="tpu_custom_call" | custom-call | tf_op jit(solution)/shard_map/grid/pallas_call | solution.py:378
  74.9 27.0 %all_to_all.21.tiles_ref = bf16[1344,2,128]{2,1,0:T(2,128)(2,1)S(1)} all-to-all(bf16[1344,2,128]{2,1,0:T(2,128)(2,1)S(1)} %grid.1), channel_id=1, replica_groups=mesh['ma'=12,'row'=64] {'row'}, dimensions={0} | all-to-all | bytes 1376256 | tf_op jit(solution)/shard_map/all_to_all | solution.py:480
  101.9 1.1 return.1
  103.0 3.5 %all-to-all-start.3 = ((bf16[12,88,128]{2,1,0:T(8,128)(2,1)}), bf16[12,88,128]{2,1,0:T(8,128)(2,1)S(1)}, u32[]{:S(2)}, u32[]{:S(2)}) async-start(bf16[12,88,128]{2,1,0:T(8,128)(2,1)} %return.1), calls=%async_computation.3 | async-start | bytes 540672 | tf_op jit(solution)/shard_map/all_to_all | solution.py:498
  106.5 0.8 flux.1
  107.3 14.3 %all-to-all-done.3.rows_ref = bf16[12,88,128]{2,1,0:T(8,128)(2,1)S(1)} async-done(((bf16[12,88,128]{2,1,0:T(8,128)(2,1)}), bf16[12,88,128]{2,1,0:T(8,128)(2,1)S(1)}, u32[]{:S(2)}, u32[]{:S(2)}) %all-to-all-start.3) | async-done | bytes 270368 | tf_op jit(solution)/shard_map/all_to_all | solution.py:498
  121.6 0.0 copy-done.2
  121.6 6.1 %analysis.1 = f32[44,2,513]{2,1,0:T(2,128)} custom-call(s32[264]{0:T(512)} %pairs_ref.3, bf16[22,513,384]{2,1,0:T(8,128)(2,1)} %source_ref.3, bf16[12,88,128]{2,1,0:T(8,128)(2,1)S(1)} %all-to-all-done.3.rows_ref, s32[384]{0:T(512)S(1)} %copy-done.2), custom_call_target="tpu_custom_call" | custom-call | tf_op jit(solution)/shard_map/analysis/pallas_call | solution.py:500
  (3 shorter events, 0.0 us)
Async XLA Ops:
  0.6 25.4 %copy-start.1 = (bf16[64,128]{1,0:T(8,128)(2,1)S(1)}, bf16[64,128]{1,0:T(8,128)(2,1)}, u32[]{:S(2)}) copy-start(bf16[64,128]{1,0:T(8,128)(2,1)} %constant.33.synth_ref) | copy-start | bytes 49156
  0.6 25.4 %copy-start = (bf16[64,192]{1,0:T(8,128)(2,1)S(1)}, bf16[64,192]{1,0:T(8,128)(2,1)}, u32[]{:S(2)}) copy-start(bf16[64,192]{1,0:T(8,128)(2,1)} %constant.38.analysis_ref) | copy-start | bytes 73732
  0.7 22.9 %copy-start.3 = (s32[264]{0:T(512)S(1)}, s32[264]{0:T(512)}, u32[]{:S(2)}) copy-start(s32[264]{0:T(512)} %pairs_ref.3) | copy-start | bytes 3172
  7.8 113.8 %copy-start.2 = (s32[384]{0:T(512)S(1)}, s32[384]{0:T(512)}, u32[]{:S(2)}) copy-start(s32[384]{0:T(512)} %theta_ref.1) | copy-start | bytes 4612
  7.8 35.0 %all-to-all-start = ((bf16[12,132,128]{2,1,0:T(8,128)(2,1)}), bf16[12,132,128]{2,1,0:T(8,128)(2,1)}, u32[]{:S(2)}, u32[]{:S(2)}) async-start(bf16[12,132,128]{2,1,0:T(8,128)(2,1)} %synthesis.1), calls=%async_computation | async-start | bytes 835584 | tf_op jit(solution)/shard_map/all_to_all | solution.py:452
  103.0 18.6 %all-to-all-start.3 = ((bf16[12,88,128]{2,1,0:T(8,128)(2,1)}), bf16[12,88,128]{2,1,0:T(8,128)(2,1)S(1)}, u32[]{:S(2)}, u32[]{:S(2)}) async-start(bf16[12,88,128]{2,1,0:T(8,128)(2,1)} %return.1), calls=%async_computation.3 | async-start | bytes 540672 | tf_op jit(solution)/shard_map/all_to_all | solution.py:498

commit v7 on v6

--- a/solution.py
+++ b/solution.py
@@ -438,7 +438,7 @@
         in_specs=[smem, far, far, far],
         out_specs=far,
         scratch_shapes=[
-            pltpu.VMEM((groups, 24 * slot_dev, LANES), F32),
+            pltpu.VMEM((groups, 26 * slot_dev + 4, LANES), F32),
             pltpu.VMEM(flat.shape, F32),
             pltpu.VMEM(theta_owner.shape, jnp.int32),
             pltpu.SemaphoreType.DMA((2,)),
@@ -460,7 +460,7 @@
         "turn",
         [((theta_dev * sent, 2, LANES), BF16)],
         (rows,),
-        [pltpu.VMEM((theta_dev * sent * 2, LANES), F32)],
+        [pltpu.VMEM((theta_dev * sent * 2 + 8, LANES), F32)],
     )
     tiles = lax.all_to_all(tiles, "row", split_axis=0, concat_axis=0, tiled=True)
     taken = -(-(2 * full + 1) // 2)
@@ -471,10 +471,10 @@
         [((levels * back, 2, LANES), BF16)],
         (tiles,) + tuple(made),
         [
-            pltpu.VMEM((levels * sent * 2, LANES), F32),
+            pltpu.VMEM((levels * sent * 2 + 8, LANES), F32),
             pltpu.VMEM((3 * levels, orders), BF16),
             pltpu.VMEM((2 * levels, NPHI), BF16),
-            pltpu.VMEM((levels * back * 2, LANES), F32),
+            pltpu.VMEM((levels * back * 2 + 8, LANES), F32),
         ],
     )
     tiles = lax.all_to_all(tiles, "row", split_axis=0, concat_axis=0, tiled=True)
@@ -484,7 +484,7 @@
         [((owners, 4 * slot_dev, 2 * theta_dev), BF16)],
         (tiles,),
         [
-            pltpu.VMEM((theta_dev * taken * 2, LANES), F32),
+            pltpu.VMEM((theta_dev * taken * 2 + 8, LANES), F32),
             pltpu.VMEM((orders, 2 * theta_dev), F32),
         ],
     )

time: 130 us -> 130 us (level)
  no operation moved by 1% of the time
where the time goes in v7:
time: 130 us; the launch traced here: 128 us
  blocking collectives  54.3 us (42%)
  waiting for transfers between devices  28.9 us (22%)
  Pallas kernels  22 us (17%)
  starting transfers between devices  19.3 us (15%)
  other arithmetic  2.27 us (2%)
    all_to_all x2, blocking collectives, local(): lax.all_to_all(tiles, 'row', split_axis=0, concat_axis=0, tiled=True)  54.3 us
    all_to_all x1, starting transfers between devices, local(): lax.all_to_all(outgoing, 'ma', split_axis=0, concat_axis=0, tiled=True)  15.7 us
    all_to_all x1, waiting for transfers between devices, local(): lax.all_to_all(outgoing, 'ma', split_axis=0, concat_axis=0, tiled=True)  14.6 us
    all_to_all x1, waiting for transfers between devices, local(): lax.all_to_all(fourier, 'ma', split_axis=0, concat_axis=0, tiled=True)  14.3 us
    pallas_call x4, Pallas kernels, call(): pl.pallas_call(kernel, out_shape=tuple((pltpu.VMEM(shape, dtype) for shap...  7.92 us
    pallas_call x1, Pallas kernels, local(): pl.pallas_call(synthesis_kernel, out_shape=jax.ShapeDtypeStruct((owners,...  7.12 us
    pallas_call x1, Pallas kernels, local(): pl.pallas_call(analysis_kernel, out_shape=jax.ShapeDtypeStruct((2 * slot_...  6.14 us
    all_to_all x1, starting transfers between devices, local(): lax.all_to_all(fourier, 'ma', split_axis=0, concat_axis=0, tiled=True)  3.54 us
  transfers between devices with their start and end apart: 2, of which 2 were waited for; matrix products, arithmetic and copies ran while one was open for 2% of the time, Pallas kernels for 2%

profile of v7, /device:TPU:1, one launch (start us, length us, event | category | flops | bytes accessed | tf_op | source)
XLA Modules:
  0.0 127.9 jit_solution(8310119889011390233)
XLA Ops:
  0.6 0.0 copy-start.1
  0.6 0.0 copy-start
  0.7 0.0 copy-start.3
  0.7 7.1 %synthesis.1 = bf16[12,132,128]{2,1,0:T(8,128)(2,1)} custom-call(s32[264]{0:T(512)} %pairs_ref.3, bf16[22,513,384]{2,1,0:T(8,128)(2,1)} %source_ref.3, f32[66,2,513]{2,1,0:T(2,128)} %bitcast.8, s32[384]{0:T(512)} %theta_ref.1), custom_call_target="tpu_custom_call" | custom-call | tf_op jit(solution)/shard_map/synthesis/pallas_call | solution.py:435
  7.8 0.0 copy-start.2
  7.8 15.7 %all-to-all-start = ((bf16[12,132,128]{2,1,0:T(8,128)(2,1)}), bf16[12,132,128]{2,1,0:T(8,128)(2,1)}, u32[]{:S(2)}, u32[]{:S(2)}) async-start(bf16[12,132,128]{2,1,0:T(8,128)(2,1)} %synthesis.1), calls=%async_computation | async-start | bytes 835584 | tf_op jit(solution)/shard_map/all_to_all | solution.py:452
  23.5 0.0 copy-done.3
  23.6 0.1 reshape.33
  23.7 0.1 mul.43
  23.8 2.2 %fusion.10 = (f32[528,128]{1,0:T(8,128)S(1)}, f32[528,128]{1,0:T(8,128)S(1)}, f32[528,128]{1,0:T(8,128)S(1)}, f32[528,128]{1,0:T(8,128)S(1)}) fusion(s32[128]{0:T(128)S(1)} %iota_multiply_fusion, s32[528]{0:T(1024)S(1)} %mul.43), kind=kLoop, calls=%fused_computation.14 | loop fusion | flops 1216512 | bytes 1083968 | tf_op jit(solution)/shard_map/sin | solution.py:407
  26.1 0.0 copy-done.1
  26.1 0.0 copy-done
  26.1 2.2 %table.1 = (bf16[1056,1536]{1,0:T(8,128)(2,1)S(1)}, bf16[64,128]{1,0:T(8,128)(2,1)S(1)}, bf16[64,192]{1,0:T(8,128)(2,1)S(1)}) custom-call(f32[528,128]{1,0:T(8,128)S(1)} %get-tuple-element.21.coarse_cos_ref, f32[528,128]{1,0:T(8,128)S(1)} %get-tuple-element.20.coarse_sin_ref, f32[528,128]{1,0:T(8,128)S(1)} %get-tuple-element.23.fine_cos_ref, ...), custom_call_target="tpu_custom_call" | custom-call | tf_op jit(solution)/shard_map/table/pallas_call | solution.py:378
  28.2 14.6 %all-to-all-done.rows_ref = bf16[12,132,128]{2,1,0:T(8,128)(2,1)} async-done(((bf16[12,132,128]{2,1,0:T(8,128)(2,1)}), bf16[12,132,128]{2,1,0:T(8,128)(2,1)}, u32[]{:S(2)}, u32[]{:S(2)}) %all-to-all-start) | async-done | bytes 405536 | tf_op jit(solution)/shard_map/all_to_all | solution.py:452
  42.8 1.6 %turn.1 = bf16[832,2,128]{2,1,0:T(2,128)(2,1)S(1)} custom-call(bf16[12,132,128]{2,1,0:T(8,128)(2,1)} %all-to-all-done.rows_ref), custom_call_target="tpu_custom_call" | custom-call | tf_op jit(solution)/shard_map/turn/pallas_call | solution.py:378
  44.4 27.4 %all_to_all.20.tiles_ref = bf16[832,2,128]{2,1,0:T(2,128)(2,1)S(1)} all-to-all(bf16[832,2,128]{2,1,0:T(2,128)(2,1)S(1)} %turn.1), channel_id=1, replica_groups=mesh['ma'=12,'row'=64] {'row'}, dimensions={0} | all-to-all | bytes 851968 | tf_op jit(solution)/shard_map/all_to_all | solution.py:465
  71.8 3.1 %grid.1 = bf16[1344,2,128]{2,1,0:T(2,128)(2,1)S(1)} custom-call(bf16[832,2,128]{2,1,0:T(2,128)(2,1)S(1)} %all_to_all.20.tiles_ref, bf16[1056,1536]{1,0:T(8,128)(2,1)S(1)} %get-tuple-element.15.table_ref, bf16[64,128]{1,0:T(8,128)(2,1)S(1)} %get-tuple-element.16.synth_ref, bf16[64,192]{1,0:T(8,128)(2,1)S(1)} %get-tuple-element.17.analysis_ref), custom_call_target="tpu_custom_call" | custom-call | tf_op jit(solution)/shard_map/grid/pallas_call | solution.py:378
  74.9 27.0 %all_to_all.21.tiles_ref = bf16[1344,2,128]{2,1,0:T(2,128)(2,1)S(1)} all-to-all(bf16[1344,2,128]{2,1,0:T(2,128)(2,1)S(1)} %grid.1), channel_id=1, replica_groups=mesh['ma'=12,'row'=64] {'row'}, dimensions={0} | all-to-all | bytes 1376256 | tf_op jit(solution)/shard_map/all_to_all | solution.py:480
  101.9 1.1 return.1
  103.0 3.5 %all-to-all-start.3 = ((bf16[12,88,128]{2,1,0:T(8,128)(2,1)}), bf16[12,88,128]{2,1,0:T(8,128)(2,1)S(1)}, u32[]{:S(2)}, u32[]{:S(2)}) async-start(bf16[12,88,128]{2,1,0:T(8,128)(2,1)} %return.1), calls=%async_computation.3 | async-start | bytes 540672 | tf_op jit(solution)/shard_map/all_to_all | solution.py:498
  106.5 0.8 flux.1
  107.3 14.3 %all-to-all-done.3.rows_ref = bf16[12,88,128]{2,1,0:T(8,128)(2,1)S(1)} async-done(((bf16[12,88,128]{2,1,0:T(8,128)(2,1)}), bf16[12,88,128]{2,1,0:T(8,128)(2,1)S(1)}, u32[]{:S(2)}, u32[]{:S(2)}) %all-to-all-start.3) | async-done | bytes 270368 | tf_op jit(solution)/shard_map/all_to_all | solution.py:498
  121.6 0.0 copy-done.2
  121.6 6.1 %analysis.1 = f32[44,2,513]{2,1,0:T(2,128)} custom-call(s32[264]{0:T(512)} %pairs_ref.3, bf16[22,513,384]{2,1,0:T(8,128)(2,1)} %source_ref.3, bf16[12,88,128]{2,1,0:T(8,128)(2,1)S(1)} %all-to-all-done.3.rows_ref, s32[384]{0:T(512)S(1)} %copy-done.2), custom_call_target="tpu_custom_call" | custom-call | tf_op jit(solution)/shard_map/analysis/pallas_call | solution.py:500
  (3 shorter events, 0.0 us)
Async XLA Ops:
  0.6 25.4 %copy-start.1 = (bf16[64,128]{1,0:T(8,128)(2,1)S(1)}, bf16[64,128]{1,0:T(8,128)(2,1)}, u32[]{:S(2)}) copy-start(bf16[64,128]{1,0:T(8,128)(2,1)} %constant.33.synth_ref) | copy-start | bytes 49156
  0.6 25.4 %copy-start = (bf16[64,192]{1,0:T(8,128)(2,1)S(1)}, bf16[64,192]{1,0:T(8,128)(2,1)}, u32[]{:S(2)}) copy-start(bf16[64,192]{1,0:T(8,128)(2,1)} %constant.38.analysis_ref) | copy-start | bytes 73732
  0.7 22.9 %copy-start.3 = (s32[264]{0:T(512)S(1)}, s32[264]{0:T(512)}, u32[]{:S(2)}) copy-start(s32[264]{0:T(512)} %pairs_ref.3) | copy-start | bytes 3172
  7.8 113.8 %copy-start.2 = (s32[384]{0:T(512)S(1)}, s32[384]{0:T(512)}, u32[]{:S(2)}) copy-start(s32[384]{0:T(512)} %theta_ref.1) | copy-start | bytes 4612
  7.8 35.0 %all-to-all-start = ((bf16[12,132,128]{2,1,0:T(8,128)(2,1)}), bf16[12,132,128]{2,1,0:T(8,128)(2,1)}, u32[]{:S(2)}, u32[]{:S(2)}) async-start(bf16[12,132,128]{2,1,0:T(8,128)(2,1)} %synthesis.1), calls=%async_computation | async-start | bytes 835584 | tf_op jit(solution)/shard_map/all_to_all | solution.py:452
  103.0 18.6 %all-to-all-start.3 = ((bf16[12,88,128]{2,1,0:T(8,128)(2,1)}), bf16[12,88,128]{2,1,0:T(8,128)(2,1)S(1)}, u32[]{:S(2)}, u32[]{:S(2)}) async-start(bf16[12,88,128]{2,1,0:T(8,128)(2,1)} %return.1), calls=%async_computation.3 | async-start | bytes 540672 | tf_op jit(solution)/shard_map/all_to_all | solution.py:498
